TPU v7x, 32 devices: a whole 2x2x4 slice. The times are simulated.
32 devices in a mesh: row: 4 (over y, x), sector: 8 (over z, core).
Axes of the slice: x: 2, y: 2, z: 4, core: 2. Of those that a mesh axis runs over, the one named last changes fastest.
Arguments:
- flow: float32 [5, 16, 8, 1024], P(None, 'row', None, 'sector'), may hold values from -0.5 to 3, as said below
- geometry: float32 [5, 16, 8, 1024], P(None, 'row', None, 'sector'), may hold values from 0.01 to 1.4, as said below
- pair_sector: int32 [3], replicated, may hold values from 0 to 7
- cell_offset: int32 [3], replicated, may hold values from 0 to 127
- interp_frac: float32 [3], replicated, may hold values from 0.1 to 0.9
Outputs:
- flow_next: float32 [5, 16, 8, 1024], P(None, 'row', None, 'sector')
- rate: float32 [5, 16, 8, 1024], P(None, 'row', None, 'sector')
Inputs may be any that keep to these rules, and one draw needn't show every extreme that they name: `flow`: density 0.85 to 1.15, each velocity component of magnitude 0.3 or less, pressure 0.7 to 1.0. `geometry`: face areas 0.7 to 1.4, volumes 0.8 to 1.25, viscosity 0.01 to 0.1.
All inputs are finite; a program needn't handle non-finite values.
Results may differ from a plain program's by a relative error of at most 0.0001.
Values sent between devices are 32-bit elements; how exact they have to be, the bound alone decides.
A program may use at most 64 MiB of HBM per device.

v0:
```python
import jax
import jax.numpy as jnp
from jax import lax
from jax.sharding import PartitionSpec as P

heat_ratio = 1.4
conduction = 1.4 / 0.72
time_step = 0.12
section_weights = (0.25, 1.0 / 6.0, 0.375, 0.5, 1.0)


def extended_2(cells, sides, width, closed):
    for axis, dim in sides:
        count = lax.axis_size(axis)
        ends = count if closed else count - 1
        head = lax.slice_in_dim(cells, 0, width, axis=dim)
        tail = lax.slice_in_dim(cells, cells.shape[dim] - width, cells.shape[dim], axis=dim)
        cells = jnp.concatenate(
            [
                lax.ppermute(tail, axis, [(i, (i + 1) % count) for i in range(ends)]),
                cells,
                lax.ppermute(head, axis, [((i + 1) % count, i) for i in range(ends)]),
            ],
            axis=dim,
        )
    return cells


def shifted(value, axis, steps):
    count = lax.axis_size(axis)
    pairs = [(source, (source + steps) % count) for source in range(count)]
    return lax.ppermute(value, axis, pairs)


def primitives(fields):
    density = fields[0]
    velocity = fields[1:4] / density
    pressure = (heat_ratio - 1.0) * (fields[4] - 0.5 * jnp.sum(fields[1:4] * velocity, axis=0))
    return (density, velocity, pressure)


def physical(fields, velocity, pressure, direction):
    normal = velocity[direction]
    parts = [fields[1 + direction]]
    for component in range(3):
        term = fields[1 + component] * normal
        if component == direction:
            term = term + pressure
        parts.append(term)
    parts.append((fields[4] + pressure) * normal)
    return jnp.stack(parts)


def face_flux(left, right, geo_left, geo_right, direction):
    area = 0.5 * (geo_left[direction] + geo_right[direction])
    viscosity = 0.5 * (geo_left[4] + geo_right[4])
    dens_left, vel_left, press_left = primitives(left)
    dens_right, vel_right, press_right = primitives(right)
    speed = jnp.maximum(
        jnp.abs(vel_left[direction]) + jnp.sqrt(heat_ratio * press_left / dens_left),
        jnp.abs(vel_right[direction]) + jnp.sqrt(heat_ratio * press_right / dens_right),
    )
    convective = 0.5 * (
        physical(left, vel_left, press_left, direction)
        + physical(right, vel_right, press_right, direction)
    )
    convective = convective - 0.5 * speed * (right - left)
    delta = vel_right - vel_left
    middle = 0.5 * (vel_right + vel_left)
    heat = conduction * (press_right / dens_right - press_left / dens_left) / (heat_ratio - 1.0)
    viscous = jnp.stack(
        [jnp.zeros_like(area), delta[0], delta[1], delta[2], jnp.sum(middle * delta, axis=0) + heat]
    )
    return area * (convective - viscosity * viscous)


def sweep(extended, geo_extended, direction):
    axis_number = direction + 1
    length = extended.shape[axis_number]
    flux = face_flux(
        lax.slice_in_dim(extended, 0, length - 1, axis=axis_number),
        lax.slice_in_dim(extended, 1, length, axis=axis_number),
        lax.slice_in_dim(geo_extended, 0, length - 1, axis=axis_number),
        lax.slice_in_dim(geo_extended, 1, length, axis=axis_number),
        direction,
    )
    return lax.slice_in_dim(flux, 1, length - 1, axis=axis_number) - lax.slice_in_dim(
        flux, 0, length - 2, axis=axis_number
    )


def residual(fields, up_ghost, down_ghost, tangent_ext, geometry, geo_tangent):
    axial_ext = jnp.concatenate([up_ghost[:, None], fields, down_ghost[:, None]], axis=1)
    geo_axial = jnp.concatenate([geometry[:, :1], geometry, geometry[:, -1:]], axis=1)
    mirror = jnp.array([1.0, 1.0, -1.0, 1.0, 1.0], jnp.float32)[:, None, None, None]
    radial_ext = jnp.concatenate(
        [fields[:, :, :1] * mirror, fields, fields[:, :, -1:] * mirror], axis=2
    )
    geo_radial = jnp.concatenate([geometry[:, :, :1], geometry, geometry[:, :, -1:]], axis=2)
    total = (
        sweep(axial_ext, geo_axial, 0)
        + sweep(radial_ext, geo_radial, 1)
        + sweep(tangent_ext, geo_tangent, 2)
    )
    return -total / geometry[3]


def local(flow, geometry, pair_sector, cell_offset, interp_frac):
    row_index = lax.axis_index("row")
    row_count = lax.axis_size("row")
    sector_count = lax.axis_size("sector")
    width = flow.shape[3]
    geo_tangent = extended_2(geometry, (("sector", 3),), 1, True)
    last_plane = row_count - 2
    up_number = jnp.clip(row_index - 1, 0, last_plane)
    down_number = jnp.clip(row_index, 0, last_plane)
    up_cells = cell_offset[up_number]
    down_cells = cell_offset[down_number]
    up_weight = interp_frac[up_number]
    down_weight = interp_frac[down_number]
    up_turn = pair_sector[up_number]
    down_turn = jnp.mod(sector_count - pair_sector[down_number] - 1, sector_count)
    current = flow
    last_rate = flow
    for section_weight in section_weights:
        tangent_ext = extended_2(current, (("sector", 3),), 1, True)
        end_layers = jnp.stack([current[:, 0], current[:, -1]], axis=1)
        neighbours = extended_2(end_layers, (("row", 1),), 1, False)
        up_plane = neighbours[:, 0]
        down_plane = neighbours[:, 3]
        for bit_index in range((sector_count - 1).bit_length()):
            moved = shifted((up_plane, down_plane), "sector", -(1 << bit_index))
            take_up = up_turn // (1 << bit_index) % 2 == 1
            take_down = down_turn // (1 << bit_index) % 2 == 1
            up_plane = jnp.where(take_up, moved[0], up_plane)
            down_plane = jnp.where(take_down, moved[1], down_plane)
        following = shifted((up_plane, down_plane), "sector", -1)
        up_window = jnp.concatenate([up_plane, following[0]], axis=2)
        down_window = jnp.concatenate([down_plane, following[1]], axis=2)
        up_ghost = (1.0 - up_weight) * lax.dynamic_slice_in_dim(up_window, up_cells, width, axis=2)
        up_ghost = up_ghost + up_weight * lax.dynamic_slice_in_dim(
            up_window, up_cells + 1, width, axis=2
        )
        down_start = width - down_cells
        down_ghost = (1.0 - down_weight) * lax.dynamic_slice_in_dim(
            down_window, down_start, width, axis=2
        )
        down_ghost = down_ghost + down_weight * lax.dynamic_slice_in_dim(
            down_window, down_start - 1, width, axis=2
        )
        up_ghost = jnp.where(row_index == 0, current[:, 0], up_ghost)
        down_ghost = jnp.where(row_index == row_count - 1, current[:, -1], down_ghost)
        last_rate = residual(current, up_ghost, down_ghost, tangent_ext, geometry, geo_tangent)
        current = flow + section_weight * time_step * last_rate
    return (current, last_rate)


def solution(mesh):
    placed = (P(None, "row", None, "sector"), P(None, "row", None, "sector"), P(), P(), P())
    return jax.shard_map(
        local,
        mesh=mesh,
        in_specs=placed,
        out_specs=(P(None, "row", None, "sector"), P(None, "row", None, "sector")),
        check_vma=False,
    )
```

profile of v0, /device:TPU:0, one launch (start us, length us, event | category | flops | bytes accessed | tf_op | source)
XLA Modules:
  0.0 178.1 jit_solution(5701880750868807799)
XLA Ops:
  1.7 4.6 %collective-permute-start.13 = (f32[5,4,8,1]{3,2,1,0:T(8,128)S(1)}, f32[5,4,8,1]{3,2,1,0:T(8,128)S(1)}, u32[]{:S(2)}, u32[]{:S(2)}) collective-permute-start(f32[5,4,8,1]{3,2,1,0:T(8,128)S(1)} %get-tuple-element.344), channel_id=1, source_target_pairs={{1,0},{2,1},{3,2},{4,3},{5,4},{6,5},{7,6},{0,7},{9,8},{10,9},{11,1... | collective-permute-start | bytes 1928 | tf_op jit(solution)/shard_map/ppermute | solution.py:22
  6.4 3.6 %collective-permute-start.11 = (f32[5,4,8,1]{3,2,1,0:T(8,128)S(1)}, f32[5,4,8,1]{3,2,1,0:T(8,128)S(1)}, u32[]{:S(2)}, u32[]{:S(2)}) collective-permute-start(f32[5,4,8,1]{3,2,1,0:T(8,128)S(1)} %get-tuple-element.342), channel_id=1, source_target_pairs={{1,0},{2,1},{3,2},{4,3},{5,4},{6,5},{7,6},{0,7},{9,8},{10,9},{11,1... | collective-permute-start | bytes 1928 | tf_op jit(solution)/shard_map/ppermute | solution.py:22
  10.0 3.4 %collective-permute-start = (f32[5,1,8,128]{3,2,0,1:T(8,128)S(1)}, f32[5,1,8,128]{3,2,0,1:T(8,128)S(1)}, u32[]{:S(2)}, u32[]{:S(2)}) collective-permute-start(f32[5,1,8,128]{3,2,0,1:T(8,128)S(1)} %get-tuple-element.332), channel_id=1, source_target_pairs={{0,8},{8,16},{16,24},{1,9},{9,17},{17,25},{2,10},{10,18},{18,26},{... | collective-permute-start | bytes 61448 | tf_op jit(solution)/shard_map/ppermute | solution.py:20
  28.8 3.3 %collective-permute-start.1 = (f32[5,8,128]{2,1,0:T(8,128)S(1)}, f32[5,8,128]{2,1,0:T(8,128)S(1)}, u32[]{:S(2)}, u32[]{:S(2)}) collective-permute-start(f32[5,8,128]{2,1,0:T(8,128)S(1)} %bitcast.344), channel_id=1, source_target_pairs={{0,7},{1,0},{2,1},{3,2},{4,3},{5,4},{6,5},{7,6},{8,15},{9,8},{10,9... | collective-permute-start | bytes 61448 | tf_op jit(solution)/shard_map/ppermute | solution.py:32
  32.4 2.1 %collective-permute-start.6 = (f32[5,8,128]{2,1,0:T(8,128)S(1)}, f32[5,8,128]{2,1,0:T(8,128)S(1)}, u32[]{:S(2)}, u32[]{:S(2)}) collective-permute-start(f32[5,8,128]{2,1,0:T(8,128)S(1)} %bitcast.353), channel_id=1, source_target_pairs={{0,7},{1,0},{2,1},{3,2},{4,3},{5,4},{6,5},{7,6},{8,15},{9,8},{10,9... | collective-permute-start | bytes 61448 | tf_op jit(solution)/shard_map/ppermute | solution.py:32
  36.0 2.4 %collective-permute-done.2 = f32[5,8,128]{2,1,0:T(8,128)S(1)} collective-permute-done((f32[5,8,128]{2,1,0:T(8,128)S(1)}, f32[5,8,128]{2,1,0:T(8,128)S(1)}, u32[]{:S(2)}, u32[]{:S(2)}) %collective-permute-start.2) | collective-permute-done | bytes 20512 | tf_op jit(solution)/shard_map/ppermute | solution.py:32
  39.8 1.6 collective-permute-start.8
  41.4 1.8 %collective-permute-done.3 = f32[5,8,128]{2,1,0:T(8,128)S(1)} collective-permute-done((f32[5,8,128]{2,1,0:T(8,128)S(1)}, f32[5,8,128]{2,1,0:T(8,128)S(1)}, u32[]{:S(2)}, u32[]{:S(2)}) %collective-permute-start.3) | collective-permute-done | bytes 20512 | tf_op jit(solution)/shard_map/ppermute | solution.py:32
  43.2 1.8 %collective-permute-start.4 = (f32[5,8,128]{2,1,0:T(8,128)S(1)}, f32[5,8,128]{2,1,0:T(8,128)S(1)}, u32[]{:S(2)}, u32[]{:S(2)}) collective-permute-start(f32[5,8,128]{2,1,0:T(8,128)S(1)} %broadcast_select_fusion.29), channel_id=1, source_target_pairs={{0,7},{1,0},{2,1},{3,2},{4,3},{5,4},{6,5},{7,6},{8,15},{9,8},{10,9... | collective-permute-start | bytes 61448 | tf_op jit(solution)/shard_map/ppermute | solution.py:32
  45.1 2.5 %collective-permute-start.9 = (f32[5,8,128]{2,1,0:T(8,128)S(1)}, f32[5,8,128]{2,1,0:T(8,128)S(1)}, u32[]{:S(2)}, u32[]{:S(2)}) collective-permute-start(f32[5,8,128]{2,1,0:T(8,128)S(1)} %broadcast_select_fusion.14), channel_id=1, source_target_pairs={{0,7},{1,0},{2,1},{3,2},{4,3},{5,4},{6,5},{7,6},{8,15},{9,8},{10,9... | collective-permute-start | bytes 61448 | tf_op jit(solution)/shard_map/ppermute | solution.py:32
  49.0 1.4 fusion.341
  51.0 3.6 %collective-permute-start.25 = (f32[5,4,8,1]{3,2,1,0:T(8,128)S(1)}, f32[5,4,8,1]{3,2,1,0:T(8,128)S(1)}, u32[]{:S(2)}, u32[]{:S(2)}) collective-permute-start(f32[5,4,8,1]{3,2,1,0:T(8,128)S(1)} %get-tuple-element.324), channel_id=1, source_target_pairs={{1,0},{2,1},{3,2},{4,3},{5,4},{6,5},{7,6},{0,7},{9,8},{10,9},{11,1... | collective-permute-start | bytes 1928 | tf_op jit(solution)/shard_map/ppermute | solution.py:22
  54.8 4.3 %collective-permute-start.14 = (f32[5,1,8,128]{3,2,0,1:T(8,128)S(1)}, f32[5,1,8,128]{3,2,0,1:T(8,128)S(1)}, u32[]{:S(2)}, u32[]{:S(2)}) collective-permute-start(f32[5,1,8,128]{3,2,0,1:T(8,128)S(1)} %get-tuple-element.313), channel_id=1, source_target_pairs={{0,8},{8,16},{16,24},{1,9},{9,17},{17,25},{2,10},{10,18},{18,26},{... | collective-permute-start | bytes 61448 | tf_op jit(solution)/shard_map/ppermute | solution.py:20
  61.2 3.3 %collective-permute-start.15 = (f32[5,8,128]{2,1,0:T(8,128)S(1)}, f32[5,8,128]{2,1,0:T(8,128)S(1)}, u32[]{:S(2)}, u32[]{:S(2)}) collective-permute-start(f32[5,8,128]{2,1,0:T(8,128)S(1)} %bitcast.350), channel_id=1, source_target_pairs={{0,7},{1,0},{2,1},{3,2},{4,3},{5,4},{6,5},{7,6},{8,15},{9,8},{10,9... | collective-permute-start | bytes 61448 | tf_op jit(solution)/shard_map/ppermute | solution.py:32
  64.8 2.1 %collective-permute-start.20 = (f32[5,8,128]{2,1,0:T(8,128)S(1)}, f32[5,8,128]{2,1,0:T(8,128)S(1)}, u32[]{:S(2)}, u32[]{:S(2)}) collective-permute-start(f32[5,8,128]{2,1,0:T(8,128)S(1)} %bitcast.346), channel_id=1, source_target_pairs={{0,7},{1,0},{2,1},{3,2},{4,3},{5,4},{6,5},{7,6},{8,15},{9,8},{10,9... | collective-permute-start | bytes 61448 | tf_op jit(solution)/shard_map/ppermute | solution.py:32
  68.4 2.4 %collective-permute-done.16 = f32[5,8,128]{2,1,0:T(8,128)S(1)} collective-permute-done((f32[5,8,128]{2,1,0:T(8,128)S(1)}, f32[5,8,128]{2,1,0:T(8,128)S(1)}, u32[]{:S(2)}, u32[]{:S(2)}) %collective-permute-start.16) | collective-permute-done | bytes 20512 | tf_op jit(solution)/shard_map/ppermute | solution.py:32
  72.2 1.6 collective-permute-start.22
  73.8 1.9 %collective-permute-done.17 = f32[5,8,128]{2,1,0:T(8,128)S(1)} collective-permute-done((f32[5,8,128]{2,1,0:T(8,128)S(1)}, f32[5,8,128]{2,1,0:T(8,128)S(1)}, u32[]{:S(2)}, u32[]{:S(2)}) %collective-permute-start.17) | collective-permute-done | bytes 20512 | tf_op jit(solution)/shard_map/ppermute | solution.py:32
  75.7 1.8 %collective-permute-start.18 = (f32[5,8,128]{2,1,0:T(8,128)S(1)}, f32[5,8,128]{2,1,0:T(8,128)S(1)}, u32[]{:S(2)}, u32[]{:S(2)}) collective-permute-start(f32[5,8,128]{2,1,0:T(8,128)S(1)} %broadcast_select_fusion.28), channel_id=1, source_target_pairs={{0,7},{1,0},{2,1},{3,2},{4,3},{5,4},{6,5},{7,6},{8,15},{9,8},{10,9... | collective-permute-start | bytes 61448 | tf_op jit(solution)/shard_map/ppermute | solution.py:32
  77.5 2.4 %collective-permute-start.23 = (f32[5,8,128]{2,1,0:T(8,128)S(1)}, f32[5,8,128]{2,1,0:T(8,128)S(1)}, u32[]{:S(2)}, u32[]{:S(2)}) collective-permute-start(f32[5,8,128]{2,1,0:T(8,128)S(1)} %broadcast_select_fusion.13), channel_id=1, source_target_pairs={{0,7},{1,0},{2,1},{3,2},{4,3},{5,4},{6,5},{7,6},{8,15},{9,8},{10,9... | collective-permute-start | bytes 61448 | tf_op jit(solution)/shard_map/ppermute | solution.py:32
  83.4 3.6 %collective-permute-start.37 = (f32[5,4,8,1]{3,2,1,0:T(8,128)S(1)}, f32[5,4,8,1]{3,2,1,0:T(8,128)S(1)}, u32[]{:S(2)}, u32[]{:S(2)}) collective-permute-start(f32[5,4,8,1]{3,2,1,0:T(8,128)S(1)} %get-tuple-element.307), channel_id=1, source_target_pairs={{1,0},{2,1},{3,2},{4,3},{5,4},{6,5},{7,6},{0,7},{9,8},{10,9},{11,1... | collective-permute-start | bytes 1928 | tf_op jit(solution)/shard_map/ppermute | solution.py:22
  87.2 3.5 %collective-permute-start.26 = (f32[5,1,8,128]{3,2,0,1:T(8,128)S(1)}, f32[5,1,8,128]{3,2,0,1:T(8,128)S(1)}, u32[]{:S(2)}, u32[]{:S(2)}) collective-permute-start(f32[5,1,8,128]{3,2,0,1:T(8,128)S(1)} %get-tuple-element.296), channel_id=1, source_target_pairs={{0,8},{8,16},{16,24},{1,9},{9,17},{17,25},{2,10},{10,18},{18,26},{... | collective-permute-start | bytes 61448 | tf_op jit(solution)/shard_map/ppermute | solution.py:20
  93.2 2.8 %collective-permute-start.27 = (f32[5,8,128]{2,1,0:T(8,128)S(1)}, f32[5,8,128]{2,1,0:T(8,128)S(1)}, u32[]{:S(2)}, u32[]{:S(2)}) collective-permute-start(f32[5,8,128]{2,1,0:T(8,128)S(1)} %bitcast.351), channel_id=1, source_target_pairs={{0,7},{1,0},{2,1},{3,2},{4,3},{5,4},{6,5},{7,6},{8,15},{9,8},{10,9... | collective-permute-start | bytes 61448 | tf_op jit(solution)/shard_map/ppermute | solution.py:32
  96.4 2.1 %collective-permute-start.32 = (f32[5,8,128]{2,1,0:T(8,128)S(1)}, f32[5,8,128]{2,1,0:T(8,128)S(1)}, u32[]{:S(2)}, u32[]{:S(2)}) collective-permute-start(f32[5,8,128]{2,1,0:T(8,128)S(1)} %bitcast.347), channel_id=1, source_target_pairs={{0,7},{1,0},{2,1},{3,2},{4,3},{5,4},{6,5},{7,6},{8,15},{9,8},{10,9... | collective-permute-start | bytes 61448 | tf_op jit(solution)/shard_map/ppermute | solution.py:32
  100.0 2.4 %collective-permute-done.28 = f32[5,8,128]{2,1,0:T(8,128)S(1)} collective-permute-done((f32[5,8,128]{2,1,0:T(8,128)S(1)}, f32[5,8,128]{2,1,0:T(8,128)S(1)}, u32[]{:S(2)}, u32[]{:S(2)}) %collective-permute-start.28) | collective-permute-done | bytes 20512 | tf_op jit(solution)/shard_map/ppermute | solution.py:32
  103.8 1.6 collective-permute-start.34
  105.3 1.9 %collective-permute-done.29 = f32[5,8,128]{2,1,0:T(8,128)S(1)} collective-permute-done((f32[5,8,128]{2,1,0:T(8,128)S(1)}, f32[5,8,128]{2,1,0:T(8,128)S(1)}, u32[]{:S(2)}, u32[]{:S(2)}) %collective-permute-start.29) | collective-permute-done | bytes 20512 | tf_op jit(solution)/shard_map/ppermute | solution.py:32
  107.2 1.8 %collective-permute-start.30 = (f32[5,8,128]{2,1,0:T(8,128)S(1)}, f32[5,8,128]{2,1,0:T(8,128)S(1)}, u32[]{:S(2)}, u32[]{:S(2)}) collective-permute-start(f32[5,8,128]{2,1,0:T(8,128)S(1)} %broadcast_select_fusion.27), channel_id=1, source_target_pairs={{0,7},{1,0},{2,1},{3,2},{4,3},{5,4},{6,5},{7,6},{8,15},{9,8},{10,9... | collective-permute-start | bytes 61448 | tf_op jit(solution)/shard_map/ppermute | solution.py:32
  109.1 2.4 %collective-permute-start.35 = (f32[5,8,128]{2,1,0:T(8,128)S(1)}, f32[5,8,128]{2,1,0:T(8,128)S(1)}, u32[]{:S(2)}, u32[]{:S(2)}) collective-permute-start(f32[5,8,128]{2,1,0:T(8,128)S(1)} %broadcast_select_fusion.12), channel_id=1, source_target_pairs={{0,7},{1,0},{2,1},{3,2},{4,3},{5,4},{6,5},{7,6},{8,15},{9,8},{10,9... | collective-permute-start | bytes 61448 | tf_op jit(solution)/shard_map/ppermute | solution.py:32
  113.0 1.4 fusion.313
  115.0 3.6 %collective-permute-start.49 = (f32[5,4,8,1]{3,2,1,0:T(8,128)S(1)}, f32[5,4,8,1]{3,2,1,0:T(8,128)S(1)}, u32[]{:S(2)}, u32[]{:S(2)}) collective-permute-start(f32[5,4,8,1]{3,2,1,0:T(8,128)S(1)} %get-tuple-element.290), channel_id=1, source_target_pairs={{1,0},{2,1},{3,2},{4,3},{5,4},{6,5},{7,6},{0,7},{9,8},{10,9},{11,1... | collective-permute-start | bytes 1928 | tf_op jit(solution)/shard_map/ppermute | solution.py:22
  118.8 3.2 %collective-permute-start.38 = (f32[5,1,8,128]{3,2,0,1:T(8,128)S(1)}, f32[5,1,8,128]{3,2,0,1:T(8,128)S(1)}, u32[]{:S(2)}, u32[]{:S(2)}) collective-permute-start(f32[5,1,8,128]{3,2,0,1:T(8,128)S(1)} %get-tuple-element.279), channel_id=1, source_target_pairs={{0,8},{8,16},{16,24},{1,9},{9,17},{17,25},{2,10},{10,18},{18,26},{... | collective-permute-start | bytes 61448 | tf_op jit(solution)/shard_map/ppermute | solution.py:20
  124.8 2.6 %collective-permute-start.39 = (f32[5,8,128]{2,1,0:T(8,128)S(1)}, f32[5,8,128]{2,1,0:T(8,128)S(1)}, u32[]{:S(2)}, u32[]{:S(2)}) collective-permute-start(f32[5,8,128]{2,1,0:T(8,128)S(1)} %bitcast.352), channel_id=1, source_target_pairs={{0,7},{1,0},{2,1},{3,2},{4,3},{5,4},{6,5},{7,6},{8,15},{9,8},{10,9... | collective-permute-start | bytes 61448 | tf_op jit(solution)/shard_map/ppermute | solution.py:32
  127.7 2.1 %collective-permute-start.44 = (f32[5,8,128]{2,1,0:T(8,128)S(1)}, f32[5,8,128]{2,1,0:T(8,128)S(1)}, u32[]{:S(2)}, u32[]{:S(2)}) collective-permute-start(f32[5,8,128]{2,1,0:T(8,128)S(1)} %bitcast.348), channel_id=1, source_target_pairs={{0,7},{1,0},{2,1},{3,2},{4,3},{5,4},{6,5},{7,6},{8,15},{9,8},{10,9... | collective-permute-start | bytes 61448 | tf_op jit(solution)/shard_map/ppermute | solution.py:32
  131.3 2.4 %collective-permute-done.40 = f32[5,8,128]{2,1,0:T(8,128)S(1)} collective-permute-done((f32[5,8,128]{2,1,0:T(8,128)S(1)}, f32[5,8,128]{2,1,0:T(8,128)S(1)}, u32[]{:S(2)}, u32[]{:S(2)}) %collective-permute-start.40) | collective-permute-done | bytes 20512 | tf_op jit(solution)/shard_map/ppermute | solution.py:32
  135.1 1.6 collective-permute-start.46
  136.6 1.9 %collective-permute-done.41 = f32[5,8,128]{2,1,0:T(8,128)S(1)} collective-permute-done((f32[5,8,128]{2,1,0:T(8,128)S(1)}, f32[5,8,128]{2,1,0:T(8,128)S(1)}, u32[]{:S(2)}, u32[]{:S(2)}) %collective-permute-start.41) | collective-permute-done | bytes 20512 | tf_op jit(solution)/shard_map/ppermute | solution.py:32
  138.5 1.8 %collective-permute-start.42 = (f32[5,8,128]{2,1,0:T(8,128)S(1)}, f32[5,8,128]{2,1,0:T(8,128)S(1)}, u32[]{:S(2)}, u32[]{:S(2)}) collective-permute-start(f32[5,8,128]{2,1,0:T(8,128)S(1)} %broadcast_select_fusion.26), channel_id=1, source_target_pairs={{0,7},{1,0},{2,1},{3,2},{4,3},{5,4},{6,5},{7,6},{8,15},{9,8},{10,9... | collective-permute-start | bytes 61448 | tf_op jit(solution)/shard_map/ppermute | solution.py:32
  140.4 2.4 %collective-permute-start.47 = (f32[5,8,128]{2,1,0:T(8,128)S(1)}, f32[5,8,128]{2,1,0:T(8,128)S(1)}, u32[]{:S(2)}, u32[]{:S(2)}) collective-permute-start(f32[5,8,128]{2,1,0:T(8,128)S(1)} %broadcast_select_fusion.11), channel_id=1, source_target_pairs={{0,7},{1,0},{2,1},{3,2},{4,3},{5,4},{6,5},{7,6},{8,15},{9,8},{10,9... | collective-permute-start | bytes 61448 | tf_op jit(solution)/shard_map/ppermute | solution.py:32
  146.3 3.6 %collective-permute-start.61 = (f32[5,4,8,1]{3,2,1,0:T(8,128)S(1)}, f32[5,4,8,1]{3,2,1,0:T(8,128)S(1)}, u32[]{:S(2)}, u32[]{:S(2)}) collective-permute-start(f32[5,4,8,1]{3,2,1,0:T(8,128)S(1)} %get-tuple-element.273), channel_id=1, source_target_pairs={{1,0},{2,1},{3,2},{4,3},{5,4},{6,5},{7,6},{0,7},{9,8},{10,9},{11,1... | collective-permute-start | bytes 1928 | tf_op jit(solution)/shard_map/ppermute | solution.py:22
  150.1 3.2 %collective-permute-start.50 = (f32[5,1,8,128]{3,2,0,1:T(8,128)S(1)}, f32[5,1,8,128]{3,2,0,1:T(8,128)S(1)}, u32[]{:S(2)}, u32[]{:S(2)}) collective-permute-start(f32[5,1,8,128]{3,2,0,1:T(8,128)S(1)} %get-tuple-element.262), channel_id=1, source_target_pairs={{0,8},{8,16},{16,24},{1,9},{9,17},{17,25},{2,10},{10,18},{18,26},{... | collective-permute-start | bytes 61448 | tf_op jit(solution)/shard_map/ppermute | solution.py:20
  156.1 2.6 %collective-permute-start.51 = (f32[5,8,128]{2,1,0:T(8,128)S(1)}, f32[5,8,128]{2,1,0:T(8,128)S(1)}, u32[]{:S(2)}, u32[]{:S(2)}) collective-permute-start(f32[5,8,128]{2,1,0:T(8,128)S(1)} %bitcast.349), channel_id=1, source_target_pairs={{0,7},{1,0},{2,1},{3,2},{4,3},{5,4},{6,5},{7,6},{8,15},{9,8},{10,9... | collective-permute-start | bytes 61448 | tf_op jit(solution)/shard_map/ppermute | solution.py:32
  159.0 2.1 %collective-permute-start.56 = (f32[5,8,128]{2,1,0:T(8,128)S(1)}, f32[5,8,128]{2,1,0:T(8,128)S(1)}, u32[]{:S(2)}, u32[]{:S(2)}) collective-permute-start(f32[5,8,128]{2,1,0:T(8,128)S(1)} %bitcast.345), channel_id=1, source_target_pairs={{0,7},{1,0},{2,1},{3,2},{4,3},{5,4},{6,5},{7,6},{8,15},{9,8},{10,9... | collective-permute-start | bytes 61448 | tf_op jit(solution)/shard_map/ppermute | solution.py:32
  162.6 2.4 %collective-permute-done.52 = f32[5,8,128]{2,1,0:T(8,128)S(1)} collective-permute-done((f32[5,8,128]{2,1,0:T(8,128)S(1)}, f32[5,8,128]{2,1,0:T(8,128)S(1)}, u32[]{:S(2)}, u32[]{:S(2)}) %collective-permute-start.52) | collective-permute-done | bytes 20512 | tf_op jit(solution)/shard_map/ppermute | solution.py:32
  166.4 1.6 collective-permute-start.58
  168.0 1.9 %collective-permute-done.53 = f32[5,8,128]{2,1,0:T(8,128)S(1)} collective-permute-done((f32[5,8,128]{2,1,0:T(8,128)S(1)}, f32[5,8,128]{2,1,0:T(8,128)S(1)}, u32[]{:S(2)}, u32[]{:S(2)}) %collective-permute-start.53) | collective-permute-done | bytes 20512 | tf_op jit(solution)/shard_map/ppermute | solution.py:32
  169.9 1.8 %collective-permute-start.54 = (f32[5,8,128]{2,1,0:T(8,128)S(1)}, f32[5,8,128]{2,1,0:T(8,128)S(1)}, u32[]{:S(2)}, u32[]{:S(2)}) collective-permute-start(f32[5,8,128]{2,1,0:T(8,128)S(1)} %broadcast_select_fusion.25), channel_id=1, source_target_pairs={{0,7},{1,0},{2,1},{3,2},{4,3},{5,4},{6,5},{7,6},{8,15},{9,8},{10,9... | collective-permute-start | bytes 61448 | tf_op jit(solution)/shard_map/ppermute | solution.py:32
  171.7 2.4 %collective-permute-start.59 = (f32[5,8,128]{2,1,0:T(8,128)S(1)}, f32[5,8,128]{2,1,0:T(8,128)S(1)}, u32[]{:S(2)}, u32[]{:S(2)}) collective-permute-start(f32[5,8,128]{2,1,0:T(8,128)S(1)} %broadcast_select_fusion.10), channel_id=1, source_target_pairs={{0,7},{1,0},{2,1},{3,2},{4,3},{5,4},{6,5},{7,6},{8,15},{9,8},{10,9... | collective-permute-start | bytes 61448 | tf_op jit(solution)/shard_map/ppermute | solution.py:32
  (293 shorter events, 47.6 us)
Async XLA Ops:
  1.7 25.1 %collective-permute-start.13 = (f32[5,4,8,1]{3,2,1,0:T(8,128)S(1)}, f32[5,4,8,1]{3,2,1,0:T(8,128)S(1)}, u32[]{:S(2)}, u32[]{:S(2)}) collective-permute-start(f32[5,4,8,1]{3,2,1,0:T(8,128)S(1)} %get-tuple-element.344), channel_id=1, source_target_pairs={{1,0},{2,1},{3,2},{4,3},{5,4},{6,5},{7,6},{0,7},{9,8},{10,9},{11,1... | collective-permute-start | bytes 1928 | tf_op jit(solution)/shard_map/ppermute | solution.py:22
  6.3 21.8 %collective-permute-start.12 = (f32[5,4,8,1]{3,2,1,0:T(8,128)S(1)}, f32[5,4,8,1]{3,2,1,0:T(8,128)S(1)}, u32[]{:S(2)}, u32[]{:S(2)}) collective-permute-start(f32[5,4,8,1]{3,2,1,0:T(8,128)S(1)} %get-tuple-element.343), channel_id=1, source_target_pairs={{0,1},{1,2},{2,3},{3,4},{4,5},{5,6},{6,7},{7,0},{8,9},{9,10},{10,1... | collective-permute-start | bytes 1928 | tf_op jit(solution)/shard_map/ppermute | solution.py:20
  6.4 22.4 %collective-permute-start.11 = (f32[5,4,8,1]{3,2,1,0:T(8,128)S(1)}, f32[5,4,8,1]{3,2,1,0:T(8,128)S(1)}, u32[]{:S(2)}, u32[]{:S(2)}) collective-permute-start(f32[5,4,8,1]{3,2,1,0:T(8,128)S(1)} %get-tuple-element.342), channel_id=1, source_target_pairs={{1,0},{2,1},{3,2},{4,3},{5,4},{6,5},{7,6},{0,7},{9,8},{10,9},{11,1... | collective-permute-start | bytes 1928 | tf_op jit(solution)/shard_map/ppermute | solution.py:22
  9.9 22.1 %collective-permute-start.10 = (f32[5,4,8,1]{3,2,1,0:T(8,128)S(1)}, f32[5,4,8,1]{3,2,1,0:T(8,128)S(1)}, u32[]{:S(2)}, u32[]{:S(2)}) collective-permute-start(f32[5,4,8,1]{3,2,1,0:T(8,128)S(1)} %get-tuple-element.341), channel_id=1, source_target_pairs={{0,1},{1,2},{2,3},{3,4},{4,5},{5,6},{6,7},{7,0},{8,9},{9,10},{10,1... | collective-permute-start | bytes 1928 | tf_op jit(solution)/shard_map/ppermute | solution.py:20
  10.0 18.8 %collective-permute-start = (f32[5,1,8,128]{3,2,0,1:T(8,128)S(1)}, f32[5,1,8,128]{3,2,0,1:T(8,128)S(1)}, u32[]{:S(2)}, u32[]{:S(2)}) collective-permute-start(f32[5,1,8,128]{3,2,0,1:T(8,128)S(1)} %get-tuple-element.332), channel_id=1, source_target_pairs={{0,8},{8,16},{16,24},{1,9},{9,17},{17,25},{2,10},{10,18},{18,26},{... | collective-permute-start | bytes 61448 | tf_op jit(solution)/shard_map/ppermute | solution.py:20
  26.8 5.7 %collective-permute-start.5 = (f32[5,1,8,128]{3,2,0,1:T(8,128)S(1)}, f32[5,1,8,128]{3,2,0,1:T(8,128)S(1)}, u32[]{:S(2)}, u32[]{:S(2)}) collective-permute-start(f32[5,1,8,128]{3,2,0,1:T(8,128)S(1)} %get-tuple-element.333), channel_id=1, source_target_pairs={{8,0},{16,8},{24,16},{9,1},{17,9},{25,17},{10,2},{18,10},{26,18},{... | collective-permute-start | bytes 61448 | tf_op jit(solution)/shard_map/ppermute | solution.py:22
  28.8 5.8 %collective-permute-start.1 = (f32[5,8,128]{2,1,0:T(8,128)S(1)}, f32[5,8,128]{2,1,0:T(8,128)S(1)}, u32[]{:S(2)}, u32[]{:S(2)}) collective-permute-start(f32[5,8,128]{2,1,0:T(8,128)S(1)} %bitcast.344), channel_id=1, source_target_pairs={{0,7},{1,0},{2,1},{3,2},{4,3},{5,4},{6,5},{7,6},{8,15},{9,8},{10,9... | collective-permute-start | bytes 61448 | tf_op jit(solution)/shard_map/ppermute | solution.py:32
  34.6 3.8 %collective-permute-start.2 = (f32[5,8,128]{2,1,0:T(8,128)S(1)}, f32[5,8,128]{2,1,0:T(8,128)S(1)}, u32[]{:S(2)}, u32[]{:S(2)}) collective-permute-start(f32[5,8,128]{2,1,0:T(8,128)S(1)} %broadcast_select_fusion.19), channel_id=1, source_target_pairs={{0,6},{1,7},{2,0},{3,1},{4,2},{5,3},{6,4},{7,5},{8,14},{9,15},{10,... | collective-permute-start | bytes 61448 | tf_op jit(solution)/shard_map/ppermute | solution.py:32
  38.4 4.8 %collective-permute-start.3 = (f32[5,8,128]{2,1,0:T(8,128)S(1)}, f32[5,8,128]{2,1,0:T(8,128)S(1)}, u32[]{:S(2)}, u32[]{:S(2)}) collective-permute-start(f32[5,8,128]{2,1,0:T(8,128)S(1)} %broadcast_select_fusion.24), channel_id=1, source_target_pairs={{0,4},{1,5},{2,6},{3,7},{4,0},{5,1},{6,2},{7,3},{8,12},{9,13},{10,... | collective-permute-start | bytes 61448 | tf_op jit(solution)/shard_map/ppermute | solution.py:32
  39.8 5.2 %collective-permute-start.8 = (f32[5,8,128]{2,1,0:T(8,128)S(1)}, f32[5,8,128]{2,1,0:T(8,128)S(1)}, u32[]{:S(2)}, u32[]{:S(2)}) collective-permute-start(f32[5,8,128]{2,1,0:T(8,128)S(1)} %broadcast_select_fusion.9), channel_id=1, source_target_pairs={{0,4},{1,5},{2,6},{3,7},{4,0},{5,1},{6,2},{7,3},{8,12},{9,13},{10,... | collective-permute-start | bytes 61448 | tf_op jit(solution)/shard_map/ppermute | solution.py:32
  43.2 4.5 %collective-permute-start.4 = (f32[5,8,128]{2,1,0:T(8,128)S(1)}, f32[5,8,128]{2,1,0:T(8,128)S(1)}, u32[]{:S(2)}, u32[]{:S(2)}) collective-permute-start(f32[5,8,128]{2,1,0:T(8,128)S(1)} %broadcast_select_fusion.29), channel_id=1, source_target_pairs={{0,7},{1,0},{2,1},{3,2},{4,3},{5,4},{6,5},{7,6},{8,15},{9,8},{10,9... | collective-permute-start | bytes 61448 | tf_op jit(solution)/shard_map/ppermute | solution.py:32
  45.1 4.0 %collective-permute-start.9 = (f32[5,8,128]{2,1,0:T(8,128)S(1)}, f32[5,8,128]{2,1,0:T(8,128)S(1)}, u32[]{:S(2)}, u32[]{:S(2)}) collective-permute-start(f32[5,8,128]{2,1,0:T(8,128)S(1)} %broadcast_select_fusion.14), channel_id=1, source_target_pairs={{0,7},{1,0},{2,1},{3,2},{4,3},{5,4},{6,5},{7,6},{8,15},{9,8},{10,9... | collective-permute-start | bytes 61448 | tf_op jit(solution)/shard_map/ppermute | solution.py:32
  51.0 9.5 %collective-permute-start.25 = (f32[5,4,8,1]{3,2,1,0:T(8,128)S(1)}, f32[5,4,8,1]{3,2,1,0:T(8,128)S(1)}, u32[]{:S(2)}, u32[]{:S(2)}) collective-permute-start(f32[5,4,8,1]{3,2,1,0:T(8,128)S(1)} %get-tuple-element.324), channel_id=1, source_target_pairs={{1,0},{2,1},{3,2},{4,3},{5,4},{6,5},{7,6},{0,7},{9,8},{10,9},{11,1... | collective-permute-start | bytes 1928 | tf_op jit(solution)/shard_map/ppermute | solution.py:22
  54.6 6.0 %collective-permute-start.24 = (f32[5,4,8,1]{3,2,1,0:T(8,128)S(1)}, f32[5,4,8,1]{3,2,1,0:T(8,128)S(1)}, u32[]{:S(2)}, u32[]{:S(2)}) collective-permute-start(f32[5,4,8,1]{3,2,1,0:T(8,128)S(1)} %get-tuple-element.323), channel_id=1, source_target_pairs={{0,1},{1,2},{2,3},{3,4},{4,5},{5,6},{6,7},{7,0},{8,9},{9,10},{10,1... | collective-permute-start | bytes 1928 | tf_op jit(solution)/shard_map/ppermute | solution.py:20
  54.8 6.4 %collective-permute-start.14 = (f32[5,1,8,128]{3,2,0,1:T(8,128)S(1)}, f32[5,1,8,128]{3,2,0,1:T(8,128)S(1)}, u32[]{:S(2)}, u32[]{:S(2)}) collective-permute-start(f32[5,1,8,128]{3,2,0,1:T(8,128)S(1)} %get-tuple-element.313), channel_id=1, source_target_pairs={{0,8},{8,16},{16,24},{1,9},{9,17},{17,25},{2,10},{10,18},{18,26},{... | collective-permute-start | bytes 61448 | tf_op jit(solution)/shard_map/ppermute | solution.py:20
  59.1 5.7 %collective-permute-start.19 = (f32[5,1,8,128]{3,2,0,1:T(8,128)S(1)}, f32[5,1,8,128]{3,2,0,1:T(8,128)S(1)}, u32[]{:S(2)}, u32[]{:S(2)}) collective-permute-start(f32[5,1,8,128]{3,2,0,1:T(8,128)S(1)} %get-tuple-element.314), channel_id=1, source_target_pairs={{8,0},{16,8},{24,16},{9,1},{17,9},{25,17},{10,2},{18,10},{26,18},{... | collective-permute-start | bytes 61448 | tf_op jit(solution)/shard_map/ppermute | solution.py:22
  61.2 5.7 %collective-permute-start.15 = (f32[5,8,128]{2,1,0:T(8,128)S(1)}, f32[5,8,128]{2,1,0:T(8,128)S(1)}, u32[]{:S(2)}, u32[]{:S(2)}) collective-permute-start(f32[5,8,128]{2,1,0:T(8,128)S(1)} %bitcast.350), channel_id=1, source_target_pairs={{0,7},{1,0},{2,1},{3,2},{4,3},{5,4},{6,5},{7,6},{8,15},{9,8},{10,9... | collective-permute-start | bytes 61448 | tf_op jit(solution)/shard_map/ppermute | solution.py:32
  70.8 4.9 %collective-permute-start.17 = (f32[5,8,128]{2,1,0:T(8,128)S(1)}, f32[5,8,128]{2,1,0:T(8,128)S(1)}, u32[]{:S(2)}, u32[]{:S(2)}) collective-permute-start(f32[5,8,128]{2,1,0:T(8,128)S(1)} %broadcast_select_fusion.23), channel_id=1, source_target_pairs={{0,4},{1,5},{2,6},{3,7},{4,0},{5,1},{6,2},{7,3},{8,12},{9,13},{10,... | collective-permute-start | bytes 61448 | tf_op jit(solution)/shard_map/ppermute | solution.py:32
  72.2 5.3 %collective-permute-start.22 = (f32[5,8,128]{2,1,0:T(8,128)S(1)}, f32[5,8,128]{2,1,0:T(8,128)S(1)}, u32[]{:S(2)}, u32[]{:S(2)}) collective-permute-start(f32[5,8,128]{2,1,0:T(8,128)S(1)} %broadcast_select_fusion.8), channel_id=1, source_target_pairs={{0,4},{1,5},{2,6},{3,7},{4,0},{5,1},{6,2},{7,3},{8,12},{9,13},{10,... | collective-permute-start | bytes 61448 | tf_op jit(solution)/shard_map/ppermute | solution.py:32
  75.7 4.4 %collective-permute-start.18 = (f32[5,8,128]{2,1,0:T(8,128)S(1)}, f32[5,8,128]{2,1,0:T(8,128)S(1)}, u32[]{:S(2)}, u32[]{:S(2)}) collective-permute-start(f32[5,8,128]{2,1,0:T(8,128)S(1)} %broadcast_select_fusion.28), channel_id=1, source_target_pairs={{0,7},{1,0},{2,1},{3,2},{4,3},{5,4},{6,5},{7,6},{8,15},{9,8},{10,9... | collective-permute-start | bytes 61448 | tf_op jit(solution)/shard_map/ppermute | solution.py:32
  77.5 3.9 %collective-permute-start.23 = (f32[5,8,128]{2,1,0:T(8,128)S(1)}, f32[5,8,128]{2,1,0:T(8,128)S(1)}, u32[]{:S(2)}, u32[]{:S(2)}) collective-permute-start(f32[5,8,128]{2,1,0:T(8,128)S(1)} %broadcast_select_fusion.13), channel_id=1, source_target_pairs={{0,7},{1,0},{2,1},{3,2},{4,3},{5,4},{6,5},{7,6},{8,15},{9,8},{10,9... | collective-permute-start | bytes 61448 | tf_op jit(solution)/shard_map/ppermute | solution.py:32
  83.4 8.7 %collective-permute-start.37 = (f32[5,4,8,1]{3,2,1,0:T(8,128)S(1)}, f32[5,4,8,1]{3,2,1,0:T(8,128)S(1)}, u32[]{:S(2)}, u32[]{:S(2)}) collective-permute-start(f32[5,4,8,1]{3,2,1,0:T(8,128)S(1)} %get-tuple-element.307), channel_id=1, source_target_pairs={{1,0},{2,1},{3,2},{4,3},{5,4},{6,5},{7,6},{0,7},{9,8},{10,9},{11,1... | collective-permute-start | bytes 1928 | tf_op jit(solution)/shard_map/ppermute | solution.py:22
  87.0 5.7 %collective-permute-start.36 = (f32[5,4,8,1]{3,2,1,0:T(8,128)S(1)}, f32[5,4,8,1]{3,2,1,0:T(8,128)S(1)}, u32[]{:S(2)}, u32[]{:S(2)}) collective-permute-start(f32[5,4,8,1]{3,2,1,0:T(8,128)S(1)} %get-tuple-element.306), channel_id=1, source_target_pairs={{0,1},{1,2},{2,3},{3,4},{4,5},{5,6},{6,7},{7,0},{8,9},{9,10},{10,1... | collective-permute-start | bytes 1928 | tf_op jit(solution)/shard_map/ppermute | solution.py:20
  87.2 6.0 %collective-permute-start.26 = (f32[5,1,8,128]{3,2,0,1:T(8,128)S(1)}, f32[5,1,8,128]{3,2,0,1:T(8,128)S(1)}, u32[]{:S(2)}, u32[]{:S(2)}) collective-permute-start(f32[5,1,8,128]{3,2,0,1:T(8,128)S(1)} %get-tuple-element.296), channel_id=1, source_target_pairs={{0,8},{8,16},{16,24},{1,9},{9,17},{17,25},{2,10},{10,18},{18,26},{... | collective-permute-start | bytes 61448 | tf_op jit(solution)/shard_map/ppermute | solution.py:20
  90.7 5.7 %collective-permute-start.31 = (f32[5,1,8,128]{3,2,0,1:T(8,128)S(1)}, f32[5,1,8,128]{3,2,0,1:T(8,128)S(1)}, u32[]{:S(2)}, u32[]{:S(2)}) collective-permute-start(f32[5,1,8,128]{3,2,0,1:T(8,128)S(1)} %get-tuple-element.297), channel_id=1, source_target_pairs={{8,0},{16,8},{24,16},{9,1},{17,9},{25,17},{10,2},{18,10},{26,18},{... | collective-permute-start | bytes 61448 | tf_op jit(solution)/shard_map/ppermute | solution.py:22
  93.2 5.2 %collective-permute-start.27 = (f32[5,8,128]{2,1,0:T(8,128)S(1)}, f32[5,8,128]{2,1,0:T(8,128)S(1)}, u32[]{:S(2)}, u32[]{:S(2)}) collective-permute-start(f32[5,8,128]{2,1,0:T(8,128)S(1)} %bitcast.351), channel_id=1, source_target_pairs={{0,7},{1,0},{2,1},{3,2},{4,3},{5,4},{6,5},{7,6},{8,15},{9,8},{10,9... | collective-permute-start | bytes 61448 | tf_op jit(solution)/shard_map/ppermute | solution.py:32
  102.3 4.9 %collective-permute-start.29 = (f32[5,8,128]{2,1,0:T(8,128)S(1)}, f32[5,8,128]{2,1,0:T(8,128)S(1)}, u32[]{:S(2)}, u32[]{:S(2)}) collective-permute-start(f32[5,8,128]{2,1,0:T(8,128)S(1)} %broadcast_select_fusion.22), channel_id=1, source_target_pairs={{0,4},{1,5},{2,6},{3,7},{4,0},{5,1},{6,2},{7,3},{8,12},{9,13},{10,... | collective-permute-start | bytes 61448 | tf_op jit(solution)/shard_map/ppermute | solution.py:32
  103.8 5.3 %collective-permute-start.34 = (f32[5,8,128]{2,1,0:T(8,128)S(1)}, f32[5,8,128]{2,1,0:T(8,128)S(1)}, u32[]{:S(2)}, u32[]{:S(2)}) collective-permute-start(f32[5,8,128]{2,1,0:T(8,128)S(1)} %broadcast_select_fusion.7), channel_id=1, source_target_pairs={{0,4},{1,5},{2,6},{3,7},{4,0},{5,1},{6,2},{7,3},{8,12},{9,13},{10,... | collective-permute-start | bytes 61448 | tf_op jit(solution)/shard_map/ppermute | solution.py:32
  107.2 4.4 %collective-permute-start.30 = (f32[5,8,128]{2,1,0:T(8,128)S(1)}, f32[5,8,128]{2,1,0:T(8,128)S(1)}, u32[]{:S(2)}, u32[]{:S(2)}) collective-permute-start(f32[5,8,128]{2,1,0:T(8,128)S(1)} %broadcast_select_fusion.27), channel_id=1, source_target_pairs={{0,7},{1,0},{2,1},{3,2},{4,3},{5,4},{6,5},{7,6},{8,15},{9,8},{10,9... | collective-permute-start | bytes 61448 | tf_op jit(solution)/shard_map/ppermute | solution.py:32
  109.1 3.9 %collective-permute-start.35 = (f32[5,8,128]{2,1,0:T(8,128)S(1)}, f32[5,8,128]{2,1,0:T(8,128)S(1)}, u32[]{:S(2)}, u32[]{:S(2)}) collective-permute-start(f32[5,8,128]{2,1,0:T(8,128)S(1)} %broadcast_select_fusion.12), channel_id=1, source_target_pairs={{0,7},{1,0},{2,1},{3,2},{4,3},{5,4},{6,5},{7,6},{8,15},{9,8},{10,9... | collective-permute-start | bytes 61448 | tf_op jit(solution)/shard_map/ppermute | solution.py:32
  115.0 8.5 %collective-permute-start.49 = (f32[5,4,8,1]{3,2,1,0:T(8,128)S(1)}, f32[5,4,8,1]{3,2,1,0:T(8,128)S(1)}, u32[]{:S(2)}, u32[]{:S(2)}) collective-permute-start(f32[5,4,8,1]{3,2,1,0:T(8,128)S(1)} %get-tuple-element.290), channel_id=1, source_target_pairs={{1,0},{2,1},{3,2},{4,3},{5,4},{6,5},{7,6},{0,7},{9,8},{10,9},{11,1... | collective-permute-start | bytes 1928 | tf_op jit(solution)/shard_map/ppermute | solution.py:22
  118.5 5.7 %collective-permute-start.48 = (f32[5,4,8,1]{3,2,1,0:T(8,128)S(1)}, f32[5,4,8,1]{3,2,1,0:T(8,128)S(1)}, u32[]{:S(2)}, u32[]{:S(2)}) collective-permute-start(f32[5,4,8,1]{3,2,1,0:T(8,128)S(1)} %get-tuple-element.289), channel_id=1, source_target_pairs={{0,1},{1,2},{2,3},{3,4},{4,5},{5,6},{6,7},{7,0},{8,9},{9,10},{10,1... | collective-permute-start | bytes 1928 | tf_op jit(solution)/shard_map/ppermute | solution.py:20
  118.8 6.0 %collective-permute-start.38 = (f32[5,1,8,128]{3,2,0,1:T(8,128)S(1)}, f32[5,1,8,128]{3,2,0,1:T(8,128)S(1)}, u32[]{:S(2)}, u32[]{:S(2)}) collective-permute-start(f32[5,1,8,128]{3,2,0,1:T(8,128)S(1)} %get-tuple-element.279), channel_id=1, source_target_pairs={{0,8},{8,16},{16,24},{1,9},{9,17},{17,25},{2,10},{10,18},{18,26},{... | collective-permute-start | bytes 61448 | tf_op jit(solution)/shard_map/ppermute | solution.py:20
  122.0 5.7 %collective-permute-start.43 = (f32[5,1,8,128]{3,2,0,1:T(8,128)S(1)}, f32[5,1,8,128]{3,2,0,1:T(8,128)S(1)}, u32[]{:S(2)}, u32[]{:S(2)}) collective-permute-start(f32[5,1,8,128]{3,2,0,1:T(8,128)S(1)} %get-tuple-element.280), channel_id=1, source_target_pairs={{8,0},{16,8},{24,16},{9,1},{17,9},{25,17},{10,2},{18,10},{26,18},{... | collective-permute-start | bytes 61448 | tf_op jit(solution)/shard_map/ppermute | solution.py:22
  124.8 5.0 %collective-permute-start.39 = (f32[5,8,128]{2,1,0:T(8,128)S(1)}, f32[5,8,128]{2,1,0:T(8,128)S(1)}, u32[]{:S(2)}, u32[]{:S(2)}) collective-permute-start(f32[5,8,128]{2,1,0:T(8,128)S(1)} %bitcast.352), channel_id=1, source_target_pairs={{0,7},{1,0},{2,1},{3,2},{4,3},{5,4},{6,5},{7,6},{8,15},{9,8},{10,9... | collective-permute-start | bytes 61448 | tf_op jit(solution)/shard_map/ppermute | solution.py:32
  133.6 4.9 %collective-permute-start.41 = (f32[5,8,128]{2,1,0:T(8,128)S(1)}, f32[5,8,128]{2,1,0:T(8,128)S(1)}, u32[]{:S(2)}, u32[]{:S(2)}) collective-permute-start(f32[5,8,128]{2,1,0:T(8,128)S(1)} %broadcast_select_fusion.21), channel_id=1, source_target_pairs={{0,4},{1,5},{2,6},{3,7},{4,0},{5,1},{6,2},{7,3},{8,12},{9,13},{10,... | collective-permute-start | bytes 61448 | tf_op jit(solution)/shard_map/ppermute | solution.py:32
  135.1 5.3 %collective-permute-start.46 = (f32[5,8,128]{2,1,0:T(8,128)S(1)}, f32[5,8,128]{2,1,0:T(8,128)S(1)}, u32[]{:S(2)}, u32[]{:S(2)}) collective-permute-start(f32[5,8,128]{2,1,0:T(8,128)S(1)} %broadcast_select_fusion.6), channel_id=1, source_target_pairs={{0,4},{1,5},{2,6},{3,7},{4,0},{5,1},{6,2},{7,3},{8,12},{9,13},{10,... | collective-permute-start | bytes 61448 | tf_op jit(solution)/shard_map/ppermute | solution.py:32
  138.5 4.4 %collective-permute-start.42 = (f32[5,8,128]{2,1,0:T(8,128)S(1)}, f32[5,8,128]{2,1,0:T(8,128)S(1)}, u32[]{:S(2)}, u32[]{:S(2)}) collective-permute-start(f32[5,8,128]{2,1,0:T(8,128)S(1)} %broadcast_select_fusion.26), channel_id=1, source_target_pairs={{0,7},{1,0},{2,1},{3,2},{4,3},{5,4},{6,5},{7,6},{8,15},{9,8},{10,9... | collective-permute-start | bytes 61448 | tf_op jit(solution)/shard_map/ppermute | solution.py:32
  140.4 3.9 %collective-permute-start.47 = (f32[5,8,128]{2,1,0:T(8,128)S(1)}, f32[5,8,128]{2,1,0:T(8,128)S(1)}, u32[]{:S(2)}, u32[]{:S(2)}) collective-permute-start(f32[5,8,128]{2,1,0:T(8,128)S(1)} %broadcast_select_fusion.11), channel_id=1, source_target_pairs={{0,7},{1,0},{2,1},{3,2},{4,3},{5,4},{6,5},{7,6},{8,15},{9,8},{10,9... | collective-permute-start | bytes 61448 | tf_op jit(solution)/shard_map/ppermute | solution.py:32
  146.3 8.5 %collective-permute-start.61 = (f32[5,4,8,1]{3,2,1,0:T(8,128)S(1)}, f32[5,4,8,1]{3,2,1,0:T(8,128)S(1)}, u32[]{:S(2)}, u32[]{:S(2)}) collective-permute-start(f32[5,4,8,1]{3,2,1,0:T(8,128)S(1)} %get-tuple-element.273), channel_id=1, source_target_pairs={{1,0},{2,1},{3,2},{4,3},{5,4},{6,5},{7,6},{0,7},{9,8},{10,9},{11,1... | collective-permute-start | bytes 1928 | tf_op jit(solution)/shard_map/ppermute | solution.py:22
  149.9 5.7 %collective-permute-start.60 = (f32[5,4,8,1]{3,2,1,0:T(8,128)S(1)}, f32[5,4,8,1]{3,2,1,0:T(8,128)S(1)}, u32[]{:S(2)}, u32[]{:S(2)}) collective-permute-start(f32[5,4,8,1]{3,2,1,0:T(8,128)S(1)} %get-tuple-element.272), channel_id=1, source_target_pairs={{0,1},{1,2},{2,3},{3,4},{4,5},{5,6},{6,7},{7,0},{8,9},{9,10},{10,1... | collective-permute-start | bytes 1928 | tf_op jit(solution)/shard_map/ppermute | solution.py:20
  150.1 6.0 %collective-permute-start.50 = (f32[5,1,8,128]{3,2,0,1:T(8,128)S(1)}, f32[5,1,8,128]{3,2,0,1:T(8,128)S(1)}, u32[]{:S(2)}, u32[]{:S(2)}) collective-permute-start(f32[5,1,8,128]{3,2,0,1:T(8,128)S(1)} %get-tuple-element.262), channel_id=1, source_target_pairs={{0,8},{8,16},{16,24},{1,9},{9,17},{17,25},{2,10},{10,18},{18,26},{... | collective-permute-start | bytes 61448 | tf_op jit(solution)/shard_map/ppermute | solution.py:20
  153.3 5.7 %collective-permute-start.55 = (f32[5,1,8,128]{3,2,0,1:T(8,128)S(1)}, f32[5,1,8,128]{3,2,0,1:T(8,128)S(1)}, u32[]{:S(2)}, u32[]{:S(2)}) collective-permute-start(f32[5,1,8,128]{3,2,0,1:T(8,128)S(1)} %get-tuple-element.263), channel_id=1, source_target_pairs={{8,0},{16,8},{24,16},{9,1},{17,9},{25,17},{10,2},{18,10},{26,18},{... | collective-permute-start | bytes 61448 | tf_op jit(solution)/shard_map/ppermute | solution.py:22
  156.1 5.0 %collective-permute-start.51 = (f32[5,8,128]{2,1,0:T(8,128)S(1)}, f32[5,8,128]{2,1,0:T(8,128)S(1)}, u32[]{:S(2)}, u32[]{:S(2)}) collective-permute-start(f32[5,8,128]{2,1,0:T(8,128)S(1)} %bitcast.349), channel_id=1, source_target_pairs={{0,7},{1,0},{2,1},{3,2},{4,3},{5,4},{6,5},{7,6},{8,15},{9,8},{10,9... | collective-permute-start | bytes 61448 | tf_op jit(solution)/shard_map/ppermute | solution.py:32
  165.0 4.9 %collective-permute-start.53 = (f32[5,8,128]{2,1,0:T(8,128)S(1)}, f32[5,8,128]{2,1,0:T(8,128)S(1)}, u32[]{:S(2)}, u32[]{:S(2)}) collective-permute-start(f32[5,8,128]{2,1,0:T(8,128)S(1)} %broadcast_select_fusion.20), channel_id=1, source_target_pairs={{0,4},{1,5},{2,6},{3,7},{4,0},{5,1},{6,2},{7,3},{8,12},{9,13},{10,... | collective-permute-start | bytes 61448 | tf_op jit(solution)/shard_map/ppermute | solution.py:32
  166.4 5.3 %collective-permute-start.58 = (f32[5,8,128]{2,1,0:T(8,128)S(1)}, f32[5,8,128]{2,1,0:T(8,128)S(1)}, u32[]{:S(2)}, u32[]{:S(2)}) collective-permute-start(f32[5,8,128]{2,1,0:T(8,128)S(1)} %broadcast_select_fusion.5), channel_id=1, source_target_pairs={{0,4},{1,5},{2,6},{3,7},{4,0},{5,1},{6,2},{7,3},{8,12},{9,13},{10,... | collective-permute-start | bytes 61448 | tf_op jit(solution)/shard_map/ppermute | solution.py:32
  169.9 4.4 %collective-permute-start.54 = (f32[5,8,128]{2,1,0:T(8,128)S(1)}, f32[5,8,128]{2,1,0:T(8,128)S(1)}, u32[]{:S(2)}, u32[]{:S(2)}) collective-permute-start(f32[5,8,128]{2,1,0:T(8,128)S(1)} %broadcast_select_fusion.25), channel_id=1, source_target_pairs={{0,7},{1,0},{2,1},{3,2},{4,3},{5,4},{6,5},{7,6},{8,15},{9,8},{10,9... | collective-permute-start | bytes 61448 | tf_op jit(solution)/shard_map/ppermute | solution.py:32
  171.7 3.9 %collective-permute-start.59 = (f32[5,8,128]{2,1,0:T(8,128)S(1)}, f32[5,8,128]{2,1,0:T(8,128)S(1)}, u32[]{:S(2)}, u32[]{:S(2)}) collective-permute-start(f32[5,8,128]{2,1,0:T(8,128)S(1)} %broadcast_select_fusion.10), channel_id=1, source_target_pairs={{0,7},{1,0},{2,1},{3,2},{4,3},{5,4},{6,5},{7,6},{8,15},{9,8},{10,9... | collective-permute-start | bytes 61448 | tf_op jit(solution)/shard_map/ppermute | solution.py:32
  (20 other events, 64.2 us)
where the time goes:
time: 179 us; the launch traced here: 178 us
  starting transfers between devices  101 us (56%)
  waiting for transfers between devices  45.2 us (25%)
  other arithmetic  15.5 us (9%)
  between operations  12.1 us (7%)
  local copies, waits for them, and re-layouts  4.11 us (2%)
    ppermute x40, starting transfers between devices, shifted(): return lax.ppermute(value, axis, pairs)  54.5 us
    ppermute x40, waiting for transfers between devices, shifted(): return lax.ppermute(value, axis, pairs)  41.9 us
    ppermute x11, starting transfers between devices, extended_2(): lax.ppermute(head, axis, [((i + 1) % count, i) for i in range(ends)])  28.9 us
    ppermute x11, starting transfers between devices, extended_2(): lax.ppermute(tail, axis, [(i, (i + 1) % count) for i in range(ends)])  17.7 us
    broadcast_in_dim x5, other arithmetic, residual(): up_ghost[:, None]  7.09 us
  transfers between devices with their start and end apart: 62, of which 33 were waited for; matrix products, arithmetic and copies ran while one was open for 4% of the time, Pallas kernels for 0%

commit v1 on v0

v1 whole, which is shorter than its diff:
```python
import functools

import jax
import jax.numpy as jnp
from jax import lax
from jax.experimental import pallas as pl
from jax.experimental.pallas import tpu as pltpu
from jax.sharding import PartitionSpec as P

gamma = 1.4
heat_factor = 1.4 / 0.72 / (gamma - 1.0)
time_step = 0.12
section_weights = (0.25, 1.0 / 6.0, 0.375, 0.5, 1.0)
MESH = pl.DeviceIdType.MESH


def cell_values(fields):
    rho, m0, m1, m2, energy = fields
    inverse = 1.0 / rho
    u = (m0 * inverse, m1 * inverse, m2 * inverse)
    kinetic = m0 * u[0] + m1 * u[1] + m2 * u[2]
    pressure = (gamma - 1.0) * (energy - 0.5 * kinetic)
    temperature = pressure * inverse
    sound = jnp.sqrt(gamma * temperature)
    heat = 0.5 * (u[0] * u[0] + u[1] * u[1] + u[2] * u[2]) + heat_factor * temperature
    return (fields, u, pressure, sound, heat)


def directed(values, direction):
    fields, u, pressure, sound, heat = values
    normal = u[direction]
    flux = [fields[1 + direction]]
    for component in range(3):
        term = fields[1 + component] * normal
        flux.append(term + pressure if component == direction else term)
    flux.append((fields[4] + pressure) * normal)
    return flux, jnp.abs(normal) + sound


def face(left, right, half_area, area_mu, direction):
    flux_left, speed_left = directed(left, direction)
    flux_right, speed_right = directed(right, direction)
    speed = jnp.maximum(speed_left, speed_right)
    gradients = [None]
    for component in range(3):
        gradients.append(right[1][component] - left[1][component])
    gradients.append(right[4] - left[4])
    out = []
    for number in range(5):
        value = half_area * (
            flux_left[number]
            + flux_right[number]
            - speed * (right[0][number] - left[0][number])
        )
        if number:
            value = value - area_mu * gradients[number]
        out.append(value)
    return out


def pick(values, index):
    if isinstance(values, (tuple, list)):
        return tuple(pick(value, index) for value in values)
    return values[index]


def kernel(
    row_count, sector_count, pair_ref, cell_ref, frac_ref, flow_ref, geo_ref, next_ref, rate_ref,
    state, part, plane_up, plane_down, mate_up, mate_down, stage, ghost, edge_out, edge_left, edge_right,
    area_face, plane_send, plane_recv, mate_send, mate_recv, edge_send, edge_recv,
):
    row = lax.axis_index("row")
    sector = lax.axis_index("sector")
    chips = sector_count // 2
    chip = sector // 2
    core = lax.rem(sector, 2)
    mate = sector + 1 - 2 * core
    right = lax.rem(sector + 1, sector_count)
    left = lax.rem(sector + sector_count - 1, sector_count)
    layers, radial, width = flow_ref.shape[1:]
    last = row_count - 1

    barrier = pltpu.get_barrier_semaphore()
    for other in (left, right):
        pl.semaphore_signal(barrier, inc=1, device_id=(row, other), device_id_type=MESH)

    @pl.when(row > 0)
    def _():
        for z in range(chips):
            pl.semaphore_signal(barrier, inc=1, device_id=(row - 1, 2 * z + core), device_id_type=MESH)

    @pl.when(row < last)
    def _():
        for z in range(chips):
            pl.semaphore_signal(barrier, inc=1, device_id=(row + 1, 2 * z + core), device_id_type=MESH)

    lane2 = lax.broadcasted_iota(jnp.int32, (radial, width), 1)
    lane = lax.broadcasted_iota(jnp.int32, (layers, radial, width), 2)
    level = lax.broadcasted_iota(jnp.int32, (layers, radial, width), 1)
    flow_tiles = 5 * layers

    def packed(tiles, base, start):
        for number, tile in enumerate(tiles):
            index = number + start
            turned = pltpu.roll(tile, (2 * index + 1) % width, 1)
            base = jnp.where(lane2 // 2 == index, turned, base)
        return base

    def unpacked(ghosts, first):
        tiles = [
            pltpu.roll(ghosts, (width - 1 - 2 * (first + x)) % width, 1) for x in range(layers)
        ]
        return jnp.stack(tiles)

    geo_pack = packed(
        [geo_ref[f, x] for f in (2, 4) for x in range(layers)],
        jnp.zeros((radial, width), jnp.float32), flow_tiles,
    )
    mu = geo_ref[4]
    area0 = geo_ref[0]
    area1 = geo_ref[1]
    inverse_volume = -1.0 / geo_ref[3]
    half0 = 0.25 * (area0[:-1] + area0[1:])
    mu0 = half0 * (mu[:-1] + mu[1:])
    half1 = 0.25 * (area1 + pltpu.roll(area1, 1, 1))
    mu1 = half1 * (mu + pltpu.roll(mu, 1, 1))
    area_face[0, : layers - 1] = half0
    area_face[1, : layers - 1] = mu0
    area_face[2] = half1
    area_face[3] = mu1
    area_face[4] = area1
    area_face[5] = area1 * mu
    area_face[6] = inverse_volume
    edge_out[0] = geo_pack
    edge_out[1] = geo_pack
    state[0] = flow_ref[...]

    pl.semaphore_wait(barrier, 2 + jnp.where(row > 0, chips, 0) + jnp.where(row < last, chips, 0))

    def plane_copy(slot, up, z):
        return pltpu.make_async_remote_copy(
            src_ref=state.at[slot, :, layers - 1 if up else 0],
            dst_ref=(plane_up if up else plane_down).at[slot, chip],
            send_sem=plane_send.at[0 if up else 1, z],
            recv_sem=plane_recv.at[slot, 0 if up else 1, chip],
            device_id=(row + 1 if up else row - 1, 2 * z + core),
            device_id_type=MESH,
        )

    def plane_arrival(slot, up, z):
        buffer = plane_up if up else plane_down
        return pltpu.make_async_remote_copy(
            src_ref=buffer.at[slot, z],
            dst_ref=buffer.at[slot, z],
            send_sem=plane_send.at[0 if up else 1, z],
            recv_sem=plane_recv.at[slot, 0 if up else 1, z],
            device_id=(row - 1 if up else row + 1, 2 * z + core),
            device_id_type=MESH,
        )

    def mate_copy(slot, up):
        which = 0 if up else 1
        return pltpu.make_async_remote_copy(
            src_ref=stage.at[slot, which],
            dst_ref=(mate_up if up else mate_down).at[slot],
            send_sem=mate_send.at[which],
            recv_sem=mate_recv.at[slot, which],
            device_id=(row, mate),
            device_id_type=MESH,
        )

    def edge_copy(slot, to_right):
        which = 0 if to_right else 1
        return pltpu.make_async_remote_copy(
            src_ref=edge_out.at[slot],
            dst_ref=(edge_left if to_right else edge_right).at[slot],
            send_sem=edge_send.at[which],
            recv_sem=edge_recv.at[slot, which],
            device_id=(row, right if to_right else left),
            device_id_type=MESH,
        )

    up_number = jnp.maximum(row - 1, 0)
    down_number = jnp.minimum(row, last - 1)
    up_pair, up_cell, up_frac = pair_ref[up_number], cell_ref[up_number], frac_ref[up_number]
    down_pair, down_cell, down_frac = pair_ref[down_number], cell_ref[down_number], frac_ref[down_number]
    up_first = sector + up_pair
    up_first_mate = mate + up_pair
    down_first = sector - down_pair - 1 + sector_count
    down_first_mate = mate - down_pair - 1 + sector_count

    def own_parity(first):
        chosen = jnp.where(lax.rem(first, 2) == core, first, first + 1)
        return lax.rem(chosen, sector_count) // 2

    def chosen_plane(buffer, slot, index):
        value = buffer[slot, 0]
        for z in range(1, chips):
            value = jnp.where(index == z, buffer[slot, z], value)
        return value

    plane_lane = lax.broadcasted_iota(jnp.int32, (5, radial, width), 2)

    def section(number, carry):
        slot = lax.rem(number, 2)
        other = 1 - slot

        order = sorted(range(chips), key=lambda z: -abs(2 * z - chips + 1))

        @pl.when(row < last)
        def _():
            for z in order:
                plane_copy(slot, True, z).start()

        @pl.when(row > 0)
        def _():
            for z in order:
                plane_copy(slot, False, z).start()

        fields = tuple(state[slot, f] for f in range(5))
        edge_out[slot] = packed(
            [fields[f][x] for f in range(5) for x in range(layers)], edge_out[slot], 0
        )
        edge_copy(slot, True).start()
        edge_copy(slot, False).start()

        own = cell_values(fields)
        inner = face(
            pick(own, slice(0, layers - 1)), pick(own, slice(1, layers)),
            area_face[0, : layers - 1], area_face[1, : layers - 1], 0,
        )
        lower = cell_values(tuple(pltpu.roll(f, 1, 1) for f in fields))
        radial_low = face(lower, own, area_face[2], area_face[3], 1)
        wall_speed = jnp.abs(own[1][1]) + own[3]
        wall_even = area_face[4] * (fields[2] * own[1][1] + own[2])
        wall_odd = area_face[4] * wall_speed * fields[2] + 2.0 * area_face[5] * own[1][1]
        zero = jnp.zeros_like(wall_even)
        for f in range(5):
            hub = wall_even - wall_odd if f == 2 else zero
            casing = wall_even + wall_odd if f == 2 else zero
            upper = jnp.where(
                level == radial - 1, casing, pltpu.roll(radial_low[f], radial - 1, 1)
            )
            total = upper - jnp.where(level == 0, hub, radial_low[f])
            border = jnp.zeros((1, radial, width), jnp.float32)
            total = total + jnp.concatenate([inner[f], border], 0) - jnp.concatenate([border, inner[f]], 0)
            part[f] = total

        edge_copy(slot, True).wait_recv()
        edge_copy(slot, False).wait_recv()
        ghosts = jnp.where(lax.rem(lane2, 2) == 0, edge_left[slot], edge_right[slot])

        def neighbours(value, first):
            border = unpacked(ghosts, first)
            low = pltpu.roll(jnp.where(lane == width - 1, border, value), 1, 2)
            high = pltpu.roll(jnp.where(lane == 0, border, value), width - 1, 2)
            return low, high

        pairs = [neighbours(fields[f], f * layers) for f in range(5)]
        area2, mu2 = geo_ref[2], geo_ref[4]
        area_low, area_high = neighbours(area2, flow_tiles)
        mu_low, mu_high = neighbours(mu2, flow_tiles + layers)
        half_low = 0.25 * (area2 + area_low)
        half_high = 0.25 * (area2 + area_high)
        low = face(cell_values(tuple(p[0] for p in pairs)), own, half_low, half_low * (mu2 + mu_low), 2)
        high = face(own, cell_values(tuple(p[1] for p in pairs)), half_high, half_high * (mu2 + mu_high), 2)
        for f in range(5):
            part[f] = part[f] + (high[f] - low[f])

        @pl.when(row > 0)
        def _():
            for z in range(chips):
                plane_arrival(slot, True, z).wait_recv()
            stage[slot, 0] = chosen_plane(plane_up, slot, own_parity(up_first_mate))
            mate_copy(slot, True).start()

        @pl.when(row < last)
        def _():
            for z in range(chips):
                plane_arrival(slot, False, z).wait_recv()
            stage[slot, 1] = chosen_plane(plane_down, slot, own_parity(down_first_mate))
            mate_copy(slot, False).start()

        @pl.when(row > 0)
        def _():
            mine = chosen_plane(plane_up, slot, own_parity(up_first))
            mate_copy(slot, True).wait_recv()
            theirs = mate_up[slot]
            is_mine = lax.rem(up_first, 2) == core
            near = jnp.where(is_mine, mine, theirs)
            far = jnp.where(is_mine, theirs, mine)
            shift = lax.rem(width - up_cell, width)
            turned = jnp.where(plane_lane + up_cell < width, near, far)
            del turned
            here = jnp.where(
                plane_lane + up_cell < width, pltpu.roll(near, shift, 2), pltpu.roll(far, shift, 2)
            )
            shift = width - 1 - up_cell
            there = jnp.where(
                plane_lane + up_cell + 1 < width, pltpu.roll(near, shift, 2), pltpu.roll(far, shift, 2)
            )
            ghost[0] = (1.0 - up_frac) * here + up_frac * there

        @pl.when(row == 0)
        def _():
            ghost[0] = state[slot, :, 0]

        @pl.when(row < last)
        def _():
            mine = chosen_plane(plane_down, slot, own_parity(down_first))
            mate_copy(slot, False).wait_recv()
            theirs = mate_down[slot]
            is_mine = lax.rem(down_first, 2) == core
            near = jnp.where(is_mine, mine, theirs)
            far = jnp.where(is_mine, theirs, mine)
            here = jnp.where(
                plane_lane >= down_cell, pltpu.roll(far, down_cell, 2), pltpu.roll(near, down_cell, 2)
            )
            shift = lax.rem(down_cell + 1, width)
            there = jnp.where(
                plane_lane >= down_cell + 1, pltpu.roll(far, shift, 2), pltpu.roll(near, shift, 2)
            )
            ghost[1] = (1.0 - down_frac) * here + down_frac * there

        @pl.when(row == last)
        def _():
            ghost[1] = state[slot, :, layers - 1]

        up_cells = cell_values(tuple(ghost[0, f] for f in range(5)))
        down_cells = cell_values(tuple(ghost[1, f] for f in range(5)))
        first_cells = cell_values(tuple(state[slot, f, 0] for f in range(5)))
        last_cells = cell_values(tuple(state[slot, f, layers - 1] for f in range(5)))
        half = 0.5 * geo_ref[0, 0]
        entry = face(up_cells, first_cells, half, 2.0 * half * geo_ref[4, 0], 0)
        half = 0.5 * geo_ref[0, layers - 1]
        leave = face(last_cells, down_cells, half, 2.0 * half * geo_ref[4, layers - 1], 0)

        weight = jnp.float32(section_weights[0] * time_step)
        for index in range(1, len(section_weights)):
            weight = jnp.where(number == index, jnp.float32(section_weights[index] * time_step), weight)
        for f in range(5):
            total = part[f]
            pieces = [total[x] for x in range(layers)]
            pieces[0] = pieces[0] - entry[f]
            pieces[-1] = pieces[-1] + leave[f]
            rate = jnp.stack(pieces) * area_face[6]
            rate_ref[f] = rate
            state[other, f] = flow_ref[f] + weight * rate

        edge_copy(slot, True).wait_send()
        edge_copy(slot, False).wait_send()

        @pl.when(row < last)
        def _():
            for z in range(chips):
                plane_copy(slot, True, z).wait_send()
            mate_copy(slot, False).wait_send()

        @pl.when(row > 0)
        def _():
            for z in range(chips):
                plane_copy(slot, False, z).wait_send()
            mate_copy(slot, True).wait_send()

        return carry

    lax.fori_loop(0, len(section_weights), section, 0)
    next_ref[...] = state[len(section_weights) % 2]


def solution(mesh):
    row_count, sector_count = mesh.shape["row"], mesh.shape["sector"]

    def local(flow, geometry, pair_sector, cell_offset, interp_frac):
        _, layers, radial, width = flow.shape
        chips = sector_count // 2
        vector = pl.BlockSpec(memory_space=pltpu.VMEM)
        scalar = pl.BlockSpec(memory_space=pltpu.SMEM)
        plane = (5, radial, width)
        f32 = jnp.float32
        return pl.pallas_call(
            functools.partial(kernel, row_count, sector_count),
            out_shape=(jax.ShapeDtypeStruct(flow.shape, f32),) * 2,
            in_specs=[scalar, scalar, scalar, vector, vector],
            out_specs=(vector, vector),
            scratch_shapes=[
                pltpu.VMEM((2,) + flow.shape, f32),
                pltpu.VMEM(flow.shape, f32),
                pltpu.VMEM((2, chips) + plane, f32),
                pltpu.VMEM((2, chips) + plane, f32),
                pltpu.VMEM((2,) + plane, f32),
                pltpu.VMEM((2,) + plane, f32),
                pltpu.VMEM((2, 2) + plane, f32),
                pltpu.VMEM((2,) + plane, f32),
                pltpu.VMEM((2, radial, width), f32),
                pltpu.VMEM((2, radial, width), f32),
                pltpu.VMEM((2, radial, width), f32),
                pltpu.VMEM((7, layers, radial, width), f32),
                pltpu.SemaphoreType.DMA((2, chips)),
                pltpu.SemaphoreType.DMA((2, 2, chips)),
                pltpu.SemaphoreType.DMA((2,)),
                pltpu.SemaphoreType.DMA((2, 2)),
                pltpu.SemaphoreType.DMA((2,)),
                pltpu.SemaphoreType.DMA((2, 2)),
            ],
            compiler_params=pltpu.CompilerParams(collective_id=0, has_side_effects=True),
        )(pair_sector, cell_offset, interp_frac, flow, geometry)

    placed = P(None, "row", None, "sector")
    return jax.shard_map(
        local,
        mesh=mesh,
        in_specs=(placed, placed, P(), P(), P()),
        out_specs=(placed, placed),
        check_vma=False,
    )
```

time: 179 us -> 47 us (0.26)
  starting transfers between devices: 101 us -> 0 us
  waiting for transfers between devices: 45.2 us -> 0 us
  Pallas kernels: 0 us -> 44 us
  other arithmetic: 15.5 us -> 0 us
  between operations: 12.1 us -> 0.65 us
  local copies, waits for them, and re-layouts: 4.11 us -> 2.2 us
    ppermute x62 -> x0, starting transfers between devices: 101 us -> none  [the longest x40 54.5 us: shifted(): return lax.ppermute(value, axis, pairs)]
    ppermute x62 -> x0, waiting for transfers between devices: 45.2 us -> none  [the longest x40 41.9 us: shifted(): return lax.ppermute(value, axis, pairs)]
    pallas_call x0 -> x1, Pallas kernels: none -> 44 us  [local(): pl.pallas_call(functools.partial(kernel, row_count, sector_count), out_sh...]
    broadcast_in_dim x5 -> x0, other arithmetic: 7.09 us -> none  [residual(): up_ghost[:, None]]
    mul x38 -> x0, other arithmetic: 3.12 us -> none  [the longest x18 1.69 us: face_flux(): return area * (convective - viscosity * viscous)]
    unnamed x71 -> x0, other arithmetic: 1.79 us -> none
  transfers between devices with their start and end apart: 62 -> 0, of which waited for: 33 -> 0; matrix products, arithmetic and copies ran while one was open for 4% -> 0% of each run, Pallas kernels for 0% -> 0%
where the time goes in v1:
time: 47 us; the launch traced here: 46.8 us
  Pallas kernels  44 us (94%)
  local copies, waits for them, and re-layouts  2.2 us (5%)
  between operations  0.65 us (1%)
    pallas_call x1, Pallas kernels, local(): pl.pallas_call(functools.partial(kernel, row_count, sector_count), out_sh...  44 us
    unnamed x4, local copies, waits for them, and re-layouts  2.2 us

profile of v1, /device:TPU:0, one launch (start us, length us, event | category | flops | bytes accessed | tf_op | source)
XLA Modules:
  0.0 46.8 jit_solution(13084069812553238788)
XLA Ops:
  0.6 44.0 %shard_map.68 = (f32[5,4,8,128]{3,2,1,0:T(8,128)}, f32[5,4,8,128]{3,2,1,0:T(8,128)}) custom-call(s32[3]{0:T(128)} %pair_ref.1, s32[3]{0:T(128)} %cell_ref.1, f32[3]{0:T(128)} %frac_ref.1, f32[5,4,8,128]{3,2,1,0:T(8,128)} %flow_ref.1, f32[5,4,8,128]{3,2,1,0:T(8,128)} %geo_ref.1), custom_call_target="tpu_custom_call" | custom-call | tf_op jit(solution)/shard_map/pallas_call | solution.py:381
  44.6 0.0 copy-start
  44.6 1.6 %copy.9 = f32[5,4,8,128]{3,2,1,0:T(8,128)} copy(f32[5,4,8,128]{3,2,1,0:T(8,128)} %get-tuple-element.4) | data formatting | bytes 163840
  46.2 0.0 copy-done
  46.2 0.6 %copy.10 = f32[5,4,8,128]{3,2,1,0:T(8,128)} copy(f32[5,4,8,128]{3,2,1,0:T(8,128)S(1)} %copy-done) | data formatting | bytes 163840
Async XLA Ops:
  44.6 1.6 %copy-start = (f32[5,4,8,128]{3,2,1,0:T(8,128)S(1)}, f32[5,4,8,128]{3,2,1,0:T(8,128)}, u32[]{:S(2)}) copy-start(f32[5,4,8,128]{3,2,1,0:T(8,128)} %get-tuple-element.5) | copy-start | bytes 245764

commit v2 on v1

--- a/solution.py
+++ b/solution.py
@@ -290,8 +290,6 @@
             near = jnp.where(is_mine, mine, theirs)
             far = jnp.where(is_mine, theirs, mine)
             shift = lax.rem(width - up_cell, width)
-            turned = jnp.where(plane_lane + up_cell < width, near, far)
-            del turned
             here = jnp.where(
                 plane_lane + up_cell < width, pltpu.roll(near, shift, 2), pltpu.roll(far, shift, 2)
             )
@@ -368,6 +366,252 @@
     next_ref[...] = state[len(section_weights) % 2]
 
 
+def ring_kernel(
+    row_count, pair_ref, cell_ref, frac_ref, flow_ref, geo_ref, next_ref, rate_ref,
+    base, state, part, coef, table, up_in, down_in, low_in, high_in, ghost, back, turn,
+    all_send, all_recv, own_sem, row_send, row_recv, rad_send, rad_recv,
+):
+    row = lax.axis_index("row")
+    me = lax.axis_index("sector")
+    layers, count, width = flow_ref.shape[1:]
+    last, top = row_count - 1, count - 1
+
+    barrier = pltpu.get_barrier_semaphore()
+    for step in range(1, count):
+        other = lax.rem(me + step, count)
+        pl.semaphore_signal(barrier, inc=1, device_id=(row, other), device_id_type=MESH)
+
+    @pl.when(row > 0)
+    def _():
+        pl.semaphore_signal(barrier, inc=1, device_id=(row - 1, me), device_id_type=MESH)
+
+    @pl.when(row < last)
+    def _():
+        pl.semaphore_signal(barrier, inc=1, device_id=(row + 1, me), device_id_type=MESH)
+
+    level = lax.broadcasted_iota(jnp.int32, (layers, count, width), 1)
+    lane = lax.broadcasted_iota(jnp.int32, (layers, count, width), 2)
+    plane_lane = lax.broadcasted_iota(jnp.int32, (5, count, width), 2)
+
+    area1, mu = geo_ref[1], geo_ref[4]
+    for index, value in enumerate((area1, mu)):
+        below = jnp.where(level == 0, value, pltpu.roll(value, 1, 1))
+        above = jnp.where(level == top, value, pltpu.roll(value, count - 1, 1))
+        table[4 + 2 * index] = value + below
+        table[5 + 2 * index] = value + above
+    table[0] = geo_ref[0]
+    table[1] = geo_ref[2]
+    table[2] = mu
+    table[3] = -1.0 / geo_ref[3]
+
+    def exchange(source, target, which, step):
+        other = lax.rem(me + step, count)
+        return pltpu.make_async_remote_copy(
+            src_ref=source.at[:, :, pl.ds(other, 1)],
+            dst_ref=target.at[:, :, pl.ds(me, 1)],
+            send_sem=all_send.at[which, step],
+            recv_sem=all_recv.at[which, step],
+            device_id=(row, other),
+            device_id_type=MESH,
+        )
+
+    def arrival(target, which, step):
+        other = lax.rem(me + count - step, count)
+        return pltpu.make_async_remote_copy(
+            src_ref=target.at[:, :, pl.ds(other, 1)],
+            dst_ref=target.at[:, :, pl.ds(other, 1)],
+            send_sem=all_send.at[which, step],
+            recv_sem=all_recv.at[which, step],
+            device_id=(row, other),
+            device_id_type=MESH,
+        )
+
+    def own_piece(source, target, which):
+        return pltpu.make_async_copy(
+            source.at[:, :, pl.ds(me, 1)], target.at[:, :, pl.ds(me, 1)], own_sem.at[which]
+        )
+
+    def begin(source, target, which):
+        for step in range(1, count):
+            exchange(source, target, which, step).start()
+        own_piece(source, target, which).start()
+
+    def finish(source, target, which):
+        own_piece(source, target, which).wait()
+        for step in range(1, count):
+            arrival(target, which, step).wait_recv()
+
+    pl.semaphore_wait(barrier, top + jnp.where(row > 0, 1, 0) + jnp.where(row < last, 1, 0))
+    begin(flow_ref, base, 0)
+    begin(table, coef, 1)
+    finish(flow_ref, base, 0)
+    state[0] = base[...]
+
+    def row_copy(slot, up):
+        which = 0 if up else 1
+        return pltpu.make_async_remote_copy(
+            src_ref=state.at[slot, :, layers - 1 if up else 0],
+            dst_ref=(up_in if up else down_in).at[slot],
+            send_sem=row_send.at[which],
+            recv_sem=row_recv.at[slot, which],
+            device_id=(row + 1 if up else row - 1, me),
+            device_id_type=MESH,
+        )
+
+    def radial_copy(slot, up):
+        which = 0 if up else 1
+        return pltpu.make_async_remote_copy(
+            src_ref=state.at[slot],
+            dst_ref=(low_in if up else high_in).at[slot],
+            send_sem=rad_send.at[which],
+            recv_sem=rad_recv.at[slot, which],
+            device_id=(row, me + 1 if up else me - 1),
+            device_id_type=MESH,
+        )
+
+    def when_each(row_action, radial_action):
+        @pl.when(row < last)
+        def _():
+            row_action(True)
+
+        @pl.when(row > 0)
+        def _():
+            row_action(False)
+
+        @pl.when(me < top)
+        def _():
+            radial_action(True)
+
+        @pl.when(me > 0)
+        def _():
+            radial_action(False)
+
+    up_number = jnp.maximum(row - 1, 0)
+    down_number = jnp.minimum(row, last - 1)
+    up_pair, up_cell, up_frac = pair_ref[up_number], cell_ref[up_number], frac_ref[up_number]
+    down_pair, down_cell, down_frac = pair_ref[down_number], cell_ref[down_number], frac_ref[down_number]
+
+    def turned(value, offset):
+        sectors, cells = offset // width, lax.rem(offset, width)
+        value = pltpu.roll(value, cells, 2)
+        near = pltpu.roll(value, lax.rem(sectors, count), 1)
+        far = pltpu.roll(value, lax.rem(sectors + 1, count), 1)
+        return jnp.where(plane_lane >= cells, near, far)
+
+    annulus = count * width
+
+    def section(number, carry):
+        slot = lax.rem(number, 2)
+        other = 1 - slot
+        when_each(lambda up: row_copy(slot, up).start(), lambda up: radial_copy(slot, up).start())
+        fields = tuple(state[slot, f] for f in range(5))
+
+        @pl.when(number == 0)
+        def _():
+            finish(table, coef, 1)
+
+        own = cell_values(fields)
+        area0, area2, mu, inverse_volume = coef[0], coef[1], coef[2], coef[3]
+        half = 0.25 * (area0[:-1] + area0[1:])
+        inner = face(
+            pick(own, slice(0, layers - 1)), pick(own, slice(1, layers)),
+            half, half * (mu[:-1] + mu[1:]), 0,
+        )
+
+        def before(value):
+            moved = pltpu.roll(value, 1, 2)
+            return jnp.where(lane == 0, pltpu.roll(moved, 1, 1), moved)
+
+        def after(value):
+            moved = pltpu.roll(value, width - 1, 2)
+            return jnp.where(lane == width - 1, pltpu.roll(moved, count - 1, 1), moved)
+
+        half = 0.25 * (area2 + before(area2))
+        tangential = face(
+            cell_values(tuple(before(f) for f in fields)), own, half, half * (mu + before(mu)), 2
+        )
+        border = jnp.zeros((1, count, width), jnp.float32)
+        for f in range(5):
+            total = after(tangential[f]) - tangential[f]
+            total = total + jnp.concatenate([inner[f], border], 0) - jnp.concatenate([border, inner[f]], 0)
+            part[f] = total
+
+        @pl.when(me > 0)
+        def _():
+            radial_copy(slot, True).wait_recv()
+
+        @pl.when(me < top)
+        def _():
+            radial_copy(slot, False).wait_recv()
+
+        mirror = (fields[0], fields[1], -fields[2], fields[3], fields[4])
+        low_cells = cell_values(tuple(jnp.where(me == 0, mirror[f], low_in[slot, f]) for f in range(5)))
+        high_cells = cell_values(tuple(jnp.where(me == top, mirror[f], high_in[slot, f]) for f in range(5)))
+        half = 0.25 * coef[4]
+        low = face(low_cells, own, half, half * coef[6], 1)
+        half = 0.25 * coef[5]
+        high = face(own, high_cells, half, half * coef[7], 1)
+        for f in range(5):
+            part[f] = part[f] + (high[f] - low[f])
+
+        @pl.when(row > 0)
+        def _():
+            row_copy(slot, True).wait_recv()
+            plane = up_in[slot]
+            offset = up_pair * width + up_cell
+            here = turned(plane, annulus - offset)
+            there = turned(plane, annulus - offset - 1)
+            ghost[0] = (1.0 - up_frac) * here + up_frac * there
+
+        @pl.when(row == 0)
+        def _():
+            ghost[0] = state[slot, :, 0]
+
+        @pl.when(row < last)
+        def _():
+            row_copy(slot, False).wait_recv()
+            plane = down_in[slot]
+            offset = down_pair * width + down_cell
+            ghost[1] = (1.0 - down_frac) * turned(plane, offset) + down_frac * turned(plane, offset + 1)
+
+        @pl.when(row == last)
+        def _():
+            ghost[1] = state[slot, :, layers - 1]
+
+        up_cells = cell_values(tuple(ghost[0, f] for f in range(5)))
+        down_cells = cell_values(tuple(ghost[1, f] for f in range(5)))
+        half = 0.5 * coef[0, 0]
+        entry = face(up_cells, pick(own, 0), half, 2.0 * half * coef[2, 0], 0)
+        half = 0.5 * coef[0, layers - 1]
+        leave = face(pick(own, layers - 1), down_cells, half, 2.0 * half * coef[2, layers - 1], 0)
+
+        weight = jnp.float32(section_weights[0] * time_step)
+        for index in range(1, len(section_weights)):
+            weight = jnp.where(number == index, jnp.float32(section_weights[index] * time_step), weight)
+        for f in range(5):
+            total = part[f]
+            pieces = [total[x] for x in range(layers)]
+            pieces[0] = pieces[0] - entry[f]
+            pieces[-1] = pieces[-1] + leave[f]
+            rate = jnp.stack(pieces) * inverse_volume
+            turn[f] = rate
+            state[other, f] = base[f] + weight * rate
+
+        when_each(lambda up: row_copy(slot, up).wait_send(), lambda up: radial_copy(slot, up).wait_send())
+        return carry
+
+    lax.fori_loop(0, len(section_weights), section, 0)
+    begin(turn, back, 2)
+    finish(turn, back, 2)
+    rate = back[...]
+    rate_ref[...] = rate
+    next_ref[...] = flow_ref[...] + jnp.float32(section_weights[-1] * time_step) * rate
+    for step in range(1, count):
+        exchange(flow_ref, base, 0, step).wait_send()
+        exchange(table, coef, 1, step).wait_send()
+        exchange(turn, back, 2, step).wait_send()
+
+
 def solution(mesh):
     row_count, sector_count = mesh.shape["row"], mesh.shape["sector"]
 
@@ -378,6 +622,35 @@
         scalar = pl.BlockSpec(memory_space=pltpu.SMEM)
         plane = (5, radial, width)
         f32 = jnp.float32
+        if radial == sector_count:
+            return pl.pallas_call(
+                functools.partial(ring_kernel, row_count),
+                out_shape=(jax.ShapeDtypeStruct(flow.shape, f32),) * 2,
+                in_specs=[scalar, scalar, scalar, vector, vector],
+                out_specs=(vector, vector),
+                scratch_shapes=[
+                    pltpu.VMEM(flow.shape, f32),
+                    pltpu.VMEM((2,) + flow.shape, f32),
+                    pltpu.VMEM(flow.shape, f32),
+                    pltpu.VMEM((8,) + flow.shape[1:], f32),
+                    pltpu.VMEM((8,) + flow.shape[1:], f32),
+                    pltpu.VMEM((2,) + plane, f32),
+                    pltpu.VMEM((2,) + plane, f32),
+                    pltpu.VMEM((2,) + flow.shape, f32),
+                    pltpu.VMEM((2,) + flow.shape, f32),
+                    pltpu.VMEM((2,) + plane, f32),
+                    pltpu.VMEM(flow.shape, f32),
+                    pltpu.VMEM(flow.shape, f32),
+                    pltpu.SemaphoreType.DMA((3, sector_count)),
+                    pltpu.SemaphoreType.DMA((3, sector_count)),
+                    pltpu.SemaphoreType.DMA((3,)),
+                    pltpu.SemaphoreType.DMA((2,)),
+                    pltpu.SemaphoreType.DMA((2, 2)),
+                    pltpu.SemaphoreType.DMA((2,)),
+                    pltpu.SemaphoreType.DMA((2, 2)),
+                ],
+                compiler_params=pltpu.CompilerParams(collective_id=1, has_side_effects=True),
+            )(pair_sector, cell_offset, interp_frac, flow, geometry)
         return pl.pallas_call(
             functools.partial(kernel, row_count, sector_count),
             out_shape=(jax.ShapeDtypeStruct(flow.shape, f32),) * 2,

time: 47 us -> 36.3 us (0.77)
  Pallas kernels: 44 us -> 33.2 us
    pallas_call x1, Pallas kernels: 44 us -> 33.2 us  [local(): pl.pallas_call(functools.partial(ring_kernel, row_count), out_shape=(jax....]
where the time goes in v2:
time: 36.3 us; the launch traced here: 36.1 us
  Pallas kernels  33.2 us (91%)
  local copies, waits for them, and re-layouts  2.2 us (6%)
  between operations  0.65 us (2%)
    pallas_call x1, Pallas kernels, local(): pl.pallas_call(functools.partial(ring_kernel, row_count), out_shape=(jax....  33.2 us
    unnamed x4, local copies, waits for them, and re-layouts  2.2 us

profile of v2, /device:TPU:0, one launch (start us, length us, event | category | flops | bytes accessed | tf_op | source)
XLA Modules:
  0.0 36.1 jit_solution(14922098190064784335)
XLA Ops:
  0.6 33.2 %shard_map.68 = (f32[5,4,8,128]{3,2,1,0:T(8,128)}, f32[5,4,8,128]{3,2,1,0:T(8,128)}) custom-call(s32[3]{0:T(128)} %pair_ref.1, s32[3]{0:T(128)} %cell_ref.1, f32[3]{0:T(128)} %frac_ref.1, f32[5,4,8,128]{3,2,1,0:T(8,128)} %flow_ref.1, f32[5,4,8,128]{3,2,1,0:T(8,128)} %geo_ref.1), custom_call_target="tpu_custom_call" | custom-call | tf_op jit(solution)/shard_map/pallas_call | solution.py:626
  33.9 0.0 copy-start
  33.9 1.6 %copy.9 = f32[5,4,8,128]{3,2,1,0:T(8,128)} copy(f32[5,4,8,128]{3,2,1,0:T(8,128)} %get-tuple-element.4) | data formatting | bytes 163840
  35.5 0.0 copy-done
  35.5 0.6 %copy.10 = f32[5,4,8,128]{3,2,1,0:T(8,128)} copy(f32[5,4,8,128]{3,2,1,0:T(8,128)S(1)} %copy-done) | data formatting | bytes 163840
Async XLA Ops:
  33.9 1.6 %copy-start = (f32[5,4,8,128]{3,2,1,0:T(8,128)S(1)}, f32[5,4,8,128]{3,2,1,0:T(8,128)}, u32[]{:S(2)}) copy-start(f32[5,4,8,128]{3,2,1,0:T(8,128)} %get-tuple-element.5) | copy-start | bytes 245764

commit v3 on v2

--- a/solution.py
+++ b/solution.py
@@ -367,15 +367,19 @@
 
 
 def ring_kernel(
-    row_count, pair_ref, cell_ref, frac_ref, flow_ref, geo_ref, next_ref, rate_ref,
-    base, state, part, coef, table, up_in, down_in, low_in, high_in, ghost, back, turn,
-    all_send, all_recv, own_sem, row_send, row_recv, rad_send, rad_recv,
+    row_count, pair_ref, cell_ref, frac_ref, flow_hbm, geo_hbm, next_ref, rate_ref,
+    flow_ref, geo_ref, base, state, part, coef, table, up_in, down_in, low_in, high_in, ghost, back, turn,
+    all_send, all_recv, own_sem, load_sem, row_send, row_recv, rad_send, rad_recv,
 ):
     row = lax.axis_index("row")
     me = lax.axis_index("sector")
     layers, count, width = flow_ref.shape[1:]
     last, top = row_count - 1, count - 1
 
+    load_flow = pltpu.make_async_copy(flow_hbm, flow_ref, load_sem.at[0])
+    load_geo = pltpu.make_async_copy(geo_hbm, geo_ref, load_sem.at[1])
+    load_geo.start()
+    load_flow.start()
     barrier = pltpu.get_barrier_semaphore()
     for step in range(1, count):
         other = lax.rem(me + step, count)
@@ -389,6 +393,7 @@
     def _():
         pl.semaphore_signal(barrier, inc=1, device_id=(row + 1, me), device_id_type=MESH)
 
+    load_geo.wait()
     level = lax.broadcasted_iota(jnp.int32, (layers, count, width), 1)
     lane = lax.broadcasted_iota(jnp.int32, (layers, count, width), 2)
     plane_lane = lax.broadcasted_iota(jnp.int32, (5, count, width), 2)
@@ -441,6 +446,7 @@
         for step in range(1, count):
             arrival(target, which, step).wait_recv()
 
+    load_flow.wait()
     pl.semaphore_wait(barrier, top + jnp.where(row > 0, 1, 0) + jnp.where(row < last, 1, 0))
     begin(flow_ref, base, 0)
     begin(table, coef, 1)
@@ -619,16 +625,19 @@
         _, layers, radial, width = flow.shape
         chips = sector_count // 2
         vector = pl.BlockSpec(memory_space=pltpu.VMEM)
+        anywhere = pl.BlockSpec(memory_space=pl.ANY)
         scalar = pl.BlockSpec(memory_space=pltpu.SMEM)
         plane = (5, radial, width)
         f32 = jnp.float32
         if radial == sector_count:
             return pl.pallas_call(
                 functools.partial(ring_kernel, row_count),
-                out_shape=(jax.ShapeDtypeStruct(flow.shape, f32),) * 2,
-                in_specs=[scalar, scalar, scalar, vector, vector],
+                out_shape=(pltpu.VMEM(flow.shape, f32),) * 2,
+                in_specs=[scalar, scalar, scalar, anywhere, anywhere],
                 out_specs=(vector, vector),
                 scratch_shapes=[
+                    pltpu.VMEM(flow.shape, f32),
+                    pltpu.VMEM(flow.shape, f32),
                     pltpu.VMEM(flow.shape, f32),
                     pltpu.VMEM((2,) + flow.shape, f32),
                     pltpu.VMEM(flow.shape, f32),
@@ -644,6 +653,7 @@
                     pltpu.SemaphoreType.DMA((3, sector_count)),
                     pltpu.SemaphoreType.DMA((3, sector_count)),
                     pltpu.SemaphoreType.DMA((3,)),
+                    pltpu.SemaphoreType.DMA((2,)),
                     pltpu.SemaphoreType.DMA((2,)),
                     pltpu.SemaphoreType.DMA((2, 2)),
                     pltpu.SemaphoreType.DMA((2,)),

time: 36.3 us -> 34.4 us (0.948)
  local copies, waits for them, and re-layouts: 2.2 us -> 1.27 us
  Pallas kernels: 33.2 us -> 32.4 us
    unnamed x4 -> x2, local copies, waits for them, and re-layouts: 2.2 us -> 1.27 us
    pallas_call x1, Pallas kernels: 33.2 us -> 32.4 us  [local(): pl.pallas_call(functools.partial(ring_kernel, row_count), out_shape=(pltp...]
where the time goes in v3:
time: 34.4 us; the launch traced here: 34.3 us
  Pallas kernels  32.4 us (94%)
  local copies, waits for them, and re-layouts  1.27 us (4%)
  between operations  0.64 us (2%)
    pallas_call x1, Pallas kernels, local(): pl.pallas_call(functools.partial(ring_kernel, row_count), out_shape=(pltp...  32.4 us
    unnamed x2, local copies, waits for them, and re-layouts  1.27 us

profile of v3, /device:TPU:0, one launch (start us, length us, event | category | flops | bytes accessed | tf_op | source)
XLA Modules:
  0.0 34.3 jit_solution(14877163177910454512)
XLA Ops:
  0.6 32.4 %shard_map.68 = (f32[5,4,8,128]{3,2,1,0:T(8,128)S(1)}, f32[5,4,8,128]{3,2,1,0:T(8,128)S(1)}) custom-call(s32[3]{0:T(128)} %pair_ref.1, s32[3]{0:T(128)} %cell_ref.1, f32[3]{0:T(128)} %frac_ref.1, f32[5,4,8,128]{3,2,1,0:T(8,128)} %flow_hbm.1, f32[5,4,8,128]{3,2,1,0:T(8,128)} %geo_hbm.1), custom_call_target="tpu_custom_call" | custom-call | tf_op jit(solution)/shard_map/pallas_call | solution.py:633
  33.0 0.6 %copy.9 = f32[5,4,8,128]{3,2,1,0:T(8,128)} copy(f32[5,4,8,128]{3,2,1,0:T(8,128)S(1)} %get-tuple-element.2) | data formatting | bytes 163840
  33.6 0.6 %copy.10 = f32[5,4,8,128]{3,2,1,0:T(8,128)} copy(f32[5,4,8,128]{3,2,1,0:T(8,128)S(1)} %get-tuple-element.3) | data formatting | bytes 163840

commit v4 on v3

--- a/solution.py
+++ b/solution.py
@@ -371,7 +371,15 @@
     flow_ref, geo_ref, base, state, part, coef, table, up_in, down_in, low_in, high_in, ghost, back, turn,
     all_send, all_recv, own_sem, load_sem, row_send, row_recv, rad_send, rad_recv,
 ):
-    row = lax.axis_index("row")
+    place = lax.axis_index("row")
+
+    def snake(value):
+        if row_count % 2:
+            return value
+        half = row_count // 2
+        return jnp.where(value < half, value, row_count - 1 + half - value)
+
+    row = snake(place)
     me = lax.axis_index("sector")
     layers, count, width = flow_ref.shape[1:]
     last, top = row_count - 1, count - 1
@@ -385,13 +393,25 @@
         other = lax.rem(me + step, count)
         pl.semaphore_signal(barrier, inc=1, device_id=(row, other), device_id_type=MESH)
 
+    @pl.when(row != place)
+    def _():
+        pl.semaphore_signal(barrier, inc=1, device_id=(row, me), device_id_type=MESH)
+
+    @pl.when(me > 0)
+    def _():
+        pl.semaphore_signal(barrier, inc=1, device_id=(place, me - 1), device_id_type=MESH)
+
+    @pl.when(me < top)
+    def _():
+        pl.semaphore_signal(barrier, inc=1, device_id=(place, me + 1), device_id_type=MESH)
+
     @pl.when(row > 0)
     def _():
-        pl.semaphore_signal(barrier, inc=1, device_id=(row - 1, me), device_id_type=MESH)
+        pl.semaphore_signal(barrier, inc=1, device_id=(snake(row - 1), me), device_id_type=MESH)
 
     @pl.when(row < last)
     def _():
-        pl.semaphore_signal(barrier, inc=1, device_id=(row + 1, me), device_id_type=MESH)
+        pl.semaphore_signal(barrier, inc=1, device_id=(snake(row + 1), me), device_id_type=MESH)
 
     load_geo.wait()
     level = lax.broadcasted_iota(jnp.int32, (layers, count, width), 1)
@@ -437,17 +457,36 @@
         )
 
     def begin(source, target, which):
-        for step in range(1, count):
-            exchange(source, target, which, step).start()
-        own_piece(source, target, which).start()
+        for index in range(count):
+            step = lax.rem(jnp.where(me < count // 2, count - 1 - index, index) - me + count, count)
+
+            @pl.when(step != 0)
+            def _():
+                exchange(source, target, which, step).start()
+
+        @pl.when(row == place)
+        def _():
+            own_piece(source, target, which).start()
+
+        @pl.when(row != place)
+        def _():
+            exchange(source, target, which, 0).start()
 
     def finish(source, target, which):
-        own_piece(source, target, which).wait()
+        @pl.when(row == place)
+        def _():
+            own_piece(source, target, which).wait()
+
+        @pl.when(row != place)
+        def _():
+            arrival(target, which, 0).wait_recv()
+
         for step in range(1, count):
             arrival(target, which, step).wait_recv()
 
     load_flow.wait()
-    pl.semaphore_wait(barrier, top + jnp.where(row > 0, 1, 0) + jnp.where(row < last, 1, 0))
+    pl.semaphore_wait(barrier, top + jnp.where(row > 0, 1, 0) + jnp.where(row < last, 1, 0)
+        + jnp.where(me > 0, 1, 0) + jnp.where(me < top, 1, 0) + jnp.where(row != place, 1, 0))
     begin(flow_ref, base, 0)
     begin(table, coef, 1)
     finish(flow_ref, base, 0)
@@ -460,37 +499,42 @@
             dst_ref=(up_in if up else down_in).at[slot],
             send_sem=row_send.at[which],
             recv_sem=row_recv.at[slot, which],
-            device_id=(row + 1 if up else row - 1, me),
+            device_id=(snake(row + 1 if up else row - 1), me),
             device_id_type=MESH,
         )
 
-    def radial_copy(slot, up):
+    pieces = ((1, layers - 2), (0, 1), (layers - 1, 1))
+
+    def radial_copy(slot, up, piece):
         which = 0 if up else 1
         return pltpu.make_async_remote_copy(
-            src_ref=state.at[slot],
-            dst_ref=(low_in if up else high_in).at[slot],
-            send_sem=rad_send.at[which],
-            recv_sem=rad_recv.at[slot, which],
-            device_id=(row, me + 1 if up else me - 1),
+            src_ref=state.at[slot, :, pl.ds(*pieces[piece])],
+            dst_ref=(low_in if up else high_in).at[slot, :, pl.ds(*pieces[piece])],
+            send_sem=rad_send.at[which, piece],
+            recv_sem=rad_recv.at[slot, which, piece],
+            device_id=(place, me + 1 if up else me - 1),
             device_id_type=MESH,
         )
 
-    def when_each(row_action, radial_action):
+    def for_rows(action):
         @pl.when(row < last)
         def _():
-            row_action(True)
+            action(True)
 
         @pl.when(row > 0)
         def _():
-            row_action(False)
-
+            action(False)
+
+    def for_radial(action, chosen):
         @pl.when(me < top)
         def _():
-            radial_action(True)
+            for piece in chosen:
+                action(True, piece)
 
         @pl.when(me > 0)
         def _():
-            radial_action(False)
+            for piece in chosen:
+                action(False, piece)
 
     up_number = jnp.maximum(row - 1, 0)
     down_number = jnp.minimum(row, last - 1)
@@ -509,7 +553,6 @@
     def section(number, carry):
         slot = lax.rem(number, 2)
         other = 1 - slot
-        when_each(lambda up: row_copy(slot, up).start(), lambda up: radial_copy(slot, up).start())
         fields = tuple(state[slot, f] for f in range(5))
 
         @pl.when(number == 0)
@@ -542,23 +585,36 @@
             total = total + jnp.concatenate([inner[f], border], 0) - jnp.concatenate([border, inner[f]], 0)
             part[f] = total
 
-        @pl.when(me > 0)
-        def _():
-            radial_copy(slot, True).wait_recv()
-
-        @pl.when(me < top)
-        def _():
-            radial_copy(slot, False).wait_recv()
+        def await_radial(chosen):
+            @pl.when(me > 0)
+            def _():
+                for piece in chosen:
+                    radial_copy(slot, True, piece).wait_recv()
+
+            @pl.when(me < top)
+            def _():
+                for piece in chosen:
+                    radial_copy(slot, False, piece).wait_recv()
 
         mirror = (fields[0], fields[1], -fields[2], fields[3], fields[4])
-        low_cells = cell_values(tuple(jnp.where(me == 0, mirror[f], low_in[slot, f]) for f in range(5)))
-        high_cells = cell_values(tuple(jnp.where(me == top, mirror[f], high_in[slot, f]) for f in range(5)))
-        half = 0.25 * coef[4]
-        low = face(low_cells, own, half, half * coef[6], 1)
-        half = 0.25 * coef[5]
-        high = face(own, high_cells, half, half * coef[7], 1)
-        for f in range(5):
-            part[f] = part[f] + (high[f] - low[f])
+
+        def add_radial(x):
+            below = tuple(jnp.where(me == 0, mirror[f][x], low_in[slot, f, x]) for f in range(5))
+            above = tuple(jnp.where(me == top, mirror[f][x], high_in[slot, f, x]) for f in range(5))
+            mine = pick(own, x)
+            half = 0.25 * coef[4, x]
+            low = face(cell_values(below), mine, half, half * coef[6, x], 1)
+            half = 0.25 * coef[5, x]
+            high = face(mine, cell_values(above), half, half * coef[7, x], 1)
+            for f in range(5):
+                part[f, x] = part[f, x] + (high[f] - low[f])
+
+        weight = jnp.float32(section_weights[0] * time_step)
+        for index in range(1, len(section_weights)):
+            weight = jnp.where(number == index, jnp.float32(section_weights[index] * time_step), weight)
+        await_radial((1, 2))
+        add_radial(0)
+        add_radial(layers - 1)
 
         @pl.when(row > 0)
         def _():
@@ -591,21 +647,36 @@
         half = 0.5 * coef[0, layers - 1]
         leave = face(pick(own, layers - 1), down_cells, half, 2.0 * half * coef[2, layers - 1], 0)
 
-        weight = jnp.float32(section_weights[0] * time_step)
-        for index in range(1, len(section_weights)):
-            weight = jnp.where(number == index, jnp.float32(section_weights[index] * time_step), weight)
         for f in range(5):
-            total = part[f]
-            pieces = [total[x] for x in range(layers)]
-            pieces[0] = pieces[0] - entry[f]
-            pieces[-1] = pieces[-1] + leave[f]
-            rate = jnp.stack(pieces) * inverse_volume
-            turn[f] = rate
-            state[other, f] = base[f] + weight * rate
-
-        when_each(lambda up: row_copy(slot, up).wait_send(), lambda up: radial_copy(slot, up).wait_send())
+            for x, total in ((0, part[f, 0] - entry[f]), (layers - 1, part[f, layers - 1] + leave[f])):
+                rate = total * inverse_volume[x]
+                turn[f, x] = rate
+                state[other, f, x] = base[f, x] + weight * rate
+        for_rows(lambda up: row_copy(slot, up).wait_send())
+        for_radial(lambda up, piece: radial_copy(slot, up, piece).wait_send(), (1, 2))
+
+        @pl.when(number < len(section_weights) - 1)
+        def _():
+            for_rows(lambda up: row_copy(other, up).start())
+            for_radial(lambda up, piece: radial_copy(other, up, piece).start(), (1, 2))
+
+        inside = slice(1, layers - 1)
+        await_radial((0,))
+        add_radial(inside)
+        for f in range(5):
+            rate = part[f, inside] * inverse_volume[inside]
+            turn[f, inside] = rate
+            state[other, f, inside] = base[f, inside] + weight * rate
+        for_radial(lambda up, piece: radial_copy(slot, up, piece).wait_send(), (0,))
+
+        @pl.when(number < len(section_weights) - 1)
+        def _():
+            for_radial(lambda up, piece: radial_copy(other, up, piece).start(), (0,))
+
         return carry
 
+    for_rows(lambda up: row_copy(0, up).start())
+    for_radial(lambda up, piece: radial_copy(0, up, piece).start(), (1, 2, 0))
     lax.fori_loop(0, len(section_weights), section, 0)
     begin(turn, back, 2)
     finish(turn, back, 2)
@@ -617,6 +688,12 @@
         exchange(table, coef, 1, step).wait_send()
         exchange(turn, back, 2, step).wait_send()
 
+    @pl.when(row != place)
+    def _():
+        exchange(flow_ref, base, 0, 0).wait_send()
+        exchange(table, coef, 1, 0).wait_send()
+        exchange(turn, back, 2, 0).wait_send()
+
 
 def solution(mesh):
     row_count, sector_count = mesh.shape["row"], mesh.shape["sector"]
@@ -629,7 +706,7 @@
         scalar = pl.BlockSpec(memory_space=pltpu.SMEM)
         plane = (5, radial, width)
         f32 = jnp.float32
-        if radial == sector_count:
+        if radial == sector_count and layers > 2:
             return pl.pallas_call(
                 functools.partial(ring_kernel, row_count),
                 out_shape=(pltpu.VMEM(flow.shape, f32),) * 2,
@@ -656,8 +733,8 @@
                     pltpu.SemaphoreType.DMA((2,)),
                     pltpu.SemaphoreType.DMA((2,)),
                     pltpu.SemaphoreType.DMA((2, 2)),
-                    pltpu.SemaphoreType.DMA((2,)),
-                    pltpu.SemaphoreType.DMA((2, 2)),
+                    pltpu.SemaphoreType.DMA((2, 3)),
+                    pltpu.SemaphoreType.DMA((2, 2, 3)),
                 ],
                 compiler_params=pltpu.CompilerParams(collective_id=1, has_side_effects=True),
             )(pair_sector, cell_offset, interp_frac, flow, geometry)

time: 34.4 us -> 33.4 us (0.971)
  Pallas kernels: 32.4 us -> 31.4 us
    pallas_call x1, Pallas kernels: 32.4 us -> 31.4 us  [local(): pl.pallas_call(functools.partial(ring_kernel, row_count), out_shape=(pltp...]
where the time goes in v4:
time: 33.4 us; the launch traced here: 33.3 us
  Pallas kernels  31.4 us (94%)
  local copies, waits for them, and re-layouts  1.27 us (4%)
  between operations  0.64 us (2%)
    pallas_call x1, Pallas kernels, local(): pl.pallas_call(functools.partial(ring_kernel, row_count), out_shape=(pltp...  31.4 us
    unnamed x2, local copies, waits for them, and re-layouts  1.27 us

profile of v4, /device:TPU:0, one launch (start us, length us, event | category | flops | bytes accessed | tf_op | source)
XLA Modules:
  0.0 33.3 jit_solution(3640816808486323750)
XLA Ops:
  0.6 31.4 %shard_map.68 = (f32[5,4,8,128]{3,2,1,0:T(8,128)S(1)}, f32[5,4,8,128]{3,2,1,0:T(8,128)S(1)}) custom-call(s32[3]{0:T(128)} %pair_ref.1, s32[3]{0:T(128)} %cell_ref.1, f32[3]{0:T(128)} %frac_ref.1, f32[5,4,8,128]{3,2,1,0:T(8,128)} %flow_hbm.1, f32[5,4,8,128]{3,2,1,0:T(8,128)} %geo_hbm.1), custom_call_target="tpu_custom_call" | custom-call | tf_op jit(solution)/shard_map/pallas_call | solution.py:710
  32.0 0.6 %copy.9 = f32[5,4,8,128]{3,2,1,0:T(8,128)} copy(f32[5,4,8,128]{3,2,1,0:T(8,128)S(1)} %get-tuple-element.2) | data formatting | bytes 163840
  32.6 0.6 %copy.10 = f32[5,4,8,128]{3,2,1,0:T(8,128)} copy(f32[5,4,8,128]{3,2,1,0:T(8,128)S(1)} %get-tuple-element.3) | data formatting | bytes 163840
